TPU v7x, 128 devices: a whole 4x4x4 slice. The times are simulated.
128 devices in a mesh: row: 8 (over x_lo, z), col: 16 (over x_hi, y, core).
Axes of the slice: x: 4 (x_hi: 2, x_lo: 2; x = x_hi * 2 + x_lo), y: 4, z: 4, core: 2. Of those that a mesh axis runs over, the one named last changes fastest.
Arguments:
- layer_inputs: float32 [2048, 16384], P(('row', 'col')), may hold values from -60 to 60
Outputs:
- gram: float32 [16384, 16384], P('row', 'col')
All inputs are finite; a program needn't handle non-finite values.
Results may differ from a plain program's by a relative error of at most 0.000073.
Values sent between devices are 32-bit elements; how exact they have to be, the bound alone decides.
No kernel may reach another device: no remote copies, remote signals or barrier semaphores. Data moves between devices by JAX's collectives and lax.ppermute only.
A program may use at most 128 MiB of HBM per device.

v0:
```python
import jax
import jax.numpy as jnp
from jax import lax
from jax.sharding import PartitionSpec as P


def broadcast(block, axis, owner):
    block = jnp.where(lax.axis_index(axis) == owner, block, jnp.zeros_like(block))
    return lax.psum(block, axis)


def shards(layer_inputs):
    n_rows = lax.axis_size("row")
    n_cols = lax.axis_size("col")
    own_columns = lax.all_to_all(layer_inputs, "col", split_axis=1, concat_axis=0, tiled=True)
    whole_columns = lax.all_gather(own_columns, "row", axis=0, tiled=True)
    count_all = whole_columns.shape[0]
    factor = n_cols // n_rows
    row_index = lax.axis_index("row")
    pieces = []
    for offset in range(factor):
        pieces.append(broadcast(whole_columns, "col", row_index * factor + offset))
    row_panel = jnp.concatenate(pieces, axis=1)
    product = lax.dot_general(
        row_panel,
        whole_columns,
        (((0,), (0,)), ((), ())),
        precision=lax.Precision.HIGHEST,
        preferred_element_type=jnp.float32,
    )
    return product / count_all


def solution(mesh):
    placed = (P(("row", "col"), None),)
    return jax.shard_map(
        shards, mesh=mesh, in_specs=placed, out_specs=P("row", "col"), check_vma=False
    )
```

profile of v0, /device:TPU:0, one launch (start us, length us, event | category | flops | bytes accessed | tf_op | source)
XLA Modules:
  0.0 403.4 jit_solution(1043086083478600279)
XLA Ops:
  6.5 0.0 all-gather.2.cloned.1.call-start
  6.5 1.3 copy.6
  7.9 25.0 %all_to_all.19 = f32[16,16,1024]{2,0,1:T(8,128)} all-to-all(f32[16,16,1024]{2,0,1:T(8,128)S(1)} %bitcast.10), channel_id=1, replica_groups=mesh['row'=8,'col'=16] {'col'}, dimensions={1} | all-to-all | bytes 2097152 | tf_op jit(solution)/shard_map/all_to_all | solution.py:15
  32.9 0.0 all-gather.2.cloned.1.call-update
  32.9 0.0 all-reduce.3.cloned.1.call-start
  33.0 90.3 %all-gather.2.cloned.1.call-done = f32[2048,1024]{1,0:T(8,128)} async-done(((f32[256,1024]{1,0:T(8,128)}), f32[2048,1024]{1,0:T(8,128)}) %all-gather.2.cloned.1.call-update) | async-done | bytes 8388624 | tf_op jit(solution)/shard_map/all_gather | solution.py:16
  123.2 12.5 %broadcast_select_fusion.1 = (f32[2048,1024]{1,0:T(8,128)}, f32[2048,1024]{1,0:T(8,128)}) fusion(f32[2048,1024]{1,0:T(8,128)} %all-gather.2.cloned.1.call-done, pred[]{:T(512)S(6)} %eq.6, pred[]{:T(512)S(6)} %eq.7), kind=kLoop, calls=%fused_computation.6 | loop fusion | flops 4194304 | bytes 25165826 | tf_op jit(solution)/shard_map/jit(_where)/select_n | solution.py:8
  135.7 0.0 all-reduce.3.cloned.1.call-update
  135.8 201.1 %all-reduce.3.cloned.1.call-done = (f32[2048,1024]{1,0:T(8,128)}, f32[2048,1024]{1,0:T(8,128)}) async-done(((f32[2048,1024]{1,0:T(8,128)}, f32[2048,1024]{1,0:T(8,128)}), (f32[2048,1024]{1,0:T(8,128)}, f32[2048,1024]{1,0:T(8,128)})) %all-reduce.3.cloned.1.call-update) | async-done | bytes 16777232 | tf_op jit(solution)/shard_map/psum | solution.py:9
  336.9 59.7 %fusion.4 = f32[2048,1024]{1,0:T(8,128)} fusion(f32[2048,1024]{1,0:T(8,128)} %all-gather.2.cloned.1.call-done, f32[2048,1024]{1,0:T(8,128)} %get-tuple-element.5, f32[2048,1024]{1,0:T(8,128)} %get-tuple-element.6), kind=kOutput, calls=%fused_computation.4 | convolution fusion | flops 51545899008 | bytes 33554432 | tf_op jit(solution)/shard_map/dot_general | solution.py:24
Async XLA Ops:
  6.5 116.7 %all-gather.2.cloned.1.call-start = ((), (), s32[]{:S(2)}) async-start(), calls=%async_computation.1 | async-start | bytes 9437184 | tf_op jit(solution)/shard_map/all_gather | solution.py:16
  32.9 304.0 %all-reduce.3.cloned.1.call-start = ((), (), s32[]{:S(2)}) async-start(), calls=%async_computation.2 | async-start | bytes 33554432 | tf_op jit(solution)/shard_map/psum | solution.py:9
Sparse Core Ops, SparseCore 0:
  33.0 90.1 all-gather.1
  135.9 200.9 all-reduce.2
where the time goes:
time: 404 us; the launch traced here: 403 us
  waiting for transfers between devices  291 us (72%)
  matrix products  59.7 us (15%)
  blocking collectives  25 us (6%)
  between operations  13.4 us (3%)
  other arithmetic  12.5 us (3%)
    psum x1, waiting for transfers between devices, broadcast(): return lax.psum(block, axis)  201 us
    all_gather x1, waiting for transfers between devices, shards(): whole_columns = lax.all_gather(own_columns, 'row', axis=0, tiled=True)  90.3 us
    dot_general x1, matrix products, shards(): lax.dot_general(row_panel, whole_columns, (((0,), (0,)), ((), ())), preci...  59.7 us
    all_to_all x1, blocking collectives, shards(): lax.all_to_all(layer_inputs, 'col', split_axis=1, concat_axis=0, tiled=True)  25 us
    select_n x1, other arithmetic, broadcast(): jnp.where(lax.axis_index(axis) == owner, block, jnp.zeros_like(block))  12.5 us
  transfers between devices with their start and end apart: 2, of which 2 were waited for; matrix products, arithmetic and copies ran while one was open for 0% of the time, Pallas kernels for 0%

commit v1 on v0

v1 whole, which is shorter than its diff:
```python
import functools

import jax
import jax.numpy as jnp
from jax import lax
from jax.experimental import pallas as pl
from jax.experimental.pallas import tpu as pltpu
from jax.sharding import Mesh, PartitionSpec as P


AXES = ("xl", "z", "xh", "y", "core")


def move(value, step):
    pairs = []
    for z in range(4):
        for y in range(4):
            pairs.append((z * 8 + y * 2, z * 8 + (y + step) % 4 * 2))
            pairs.append((z * 8 + y * 2 + 1, (z + step) % 4 * 8 + y * 2 + 1))
    return lax.ppermute(value, ("z", "y", "core"), pairs)


def move_ring(value, step):
    pairs = []
    for z in range(4):
        for y in range(4):
            pairs.append((z * 8 + y * 2, (z + step) % 4 * 8 + y * 2))
            pairs.append((z * 8 + y * 2 + 1, z * 8 + (y + step) % 4 * 2 + 1))
    return lax.ppermute(value, ("z", "y", "core"), pairs)


def move_x(value, step):
    place = [0, 2, 1, 3]
    pairs = [(place[i], place[(i + step) % 4]) for i in range(4)]
    return lax.ppermute(value, ("xl", "xh"), pairs)


def swap(value):
    return lax.ppermute(value, "core", [(0, 1), (1, 0)])


def pick(value, index):
    return lax.dynamic_index_in_dim(value, index, 0, keepdims=False)


def after(values, deps):
    count = len(values)
    return lax.optimization_barrier(tuple(values) + tuple(deps))[:count]


def split(value):
    high = value.astype(jnp.bfloat16)
    return high, (value - high.astype(jnp.float32)).astype(jnp.bfloat16)


def gram_kernel(core_ref, *refs, scale, tile, last):
    mine, theirs = refs[:2]
    total = refs[2] if len(refs) == 5 else None
    out, right = refs[-2:]
    first = core_ref[0] == 0
    outer, inner, cols = mine.shape
    width, piece, count = cols // 2, inner // outer, outer * inner

    @pl.when(pl.program_id(0) == 0)
    def _():
        for i in range(outer):
            for j in range(outer):
                rows = pl.ds(j * piece, piece)
                ours, other = mine[i, rows, :width], theirs[i, rows, width:]
                high, low = split(jnp.where(first, ours, other))
                at = (j * outer + i) * piece
                right[pl.ds(at, piece), :] = high
                right[pl.ds(count + at, piece), :] = low
                right[pl.ds(2 * count + at, piece), :] = high

    at = pl.ds(pl.multiple_of(pl.program_id(0) * tile, tile), tile)
    left = jnp.where(first, theirs[:, :, at], mine[:, :, at]).reshape(count, tile).T
    high, low = split(left)
    part = jnp.dot(
        jnp.concatenate([high, high, low], axis=1),
        right[...],
        preferred_element_type=jnp.float32,
    )
    if total is not None:
        part = total[at, :] + part
    if last:
        out[...] = part * scale
    else:
        out[at, :] = part


def gram_add(core, mine, theirs, total, scale=None, tile=256):
    outer, inner, cols = mine.shape
    width, count = cols // 2, outer * inner
    whole = pl.BlockSpec(memory_space=pltpu.VMEM)
    args = [mine, theirs] + ([] if total is None else [total])
    last = scale is not None
    return pl.pallas_call(
        functools.partial(gram_kernel, scale=scale, tile=tile, last=last),
        out_shape=jax.ShapeDtypeStruct((cols, width), jnp.float32),
        grid_spec=pltpu.PrefetchScalarGridSpec(
            num_scalar_prefetch=1,
            grid=(cols // tile,),
            in_specs=[whole] * len(args),
            out_specs=pl.BlockSpec((tile, width), lambda m, c: (m, 0)) if last else whole,
            scratch_shapes=[pltpu.VMEM((3 * count, width), jnp.bfloat16)],
        ),
        input_output_aliases={} if last or total is None else {3: 0},
        compiler_params=pltpu.CompilerParams(vmem_limit_bytes=30 << 20),
        cost_estimate=pl.CostEstimate(
            flops=6 * count * cols * width, bytes_accessed=16 << 20, transcendentals=0
        ),
    )(core.reshape(1), *args)


def shards(block):
    rows, width = block.shape
    cols = width // 8
    core = lax.axis_index("core")
    first = core == 0
    y, z = lax.axis_index("y"), lax.axis_index("z")
    x = lax.axis_index("xh") * 2 + lax.axis_index("xl")

    got = swap(block)
    chip = jnp.concatenate([jnp.where(first, block, got), jnp.where(first, got, block)])

    def slab(index):
        starts = [(4 * h + index) * cols for h in (0, 1)]
        return [lax.dynamic_slice(chip, (0, s), (2 * rows, cols)) for s in starts]

    here = jnp.where(first, y, z)
    parts = [jnp.stack(slab(here))]
    for step in (1, 3, 2):
        parts.append(move(jnp.stack(slab((here + step) % 4)), step))
    parts = jnp.stack(parts, axis=1)

    def message(step):
        there = (x + step) % 4
        return pick(parts, jnp.where(first, there // 2, there % 2))

    tokens = 8 * rows
    own = message(0).reshape(1, tokens, cols)
    left = move_x(message(1), 1).reshape(1, tokens, cols)
    right = move_x(message(3), 3).reshape(1, tokens, cols)
    (second,) = after([message(2)], [left, right])
    far = move_x(second, 2).reshape(1, tokens, cols)

    def begin(value):
        return move_ring(value, 1), move_ring(value, -1)

    def forward(ahead, back):
        half = tokens // 2
        far_a = move_ring(ahead[:, :half], 1)
        far_b = move_ring(back[:, half:], -1)
        return far_a, far_b

    def finish(near, ends):
        near = jnp.concatenate(near)
        ends = jnp.concatenate(ends, axis=1)
        theirs = jnp.concatenate([swap(near), swap(ends)])
        return jnp.concatenate([near, ends]), theirs

    def gather(value, ahead, back, far_a, far_b, index):
        ends = jnp.concatenate([far_a[index], far_b[index]])
        return jnp.stack([value[index], ahead[index], back[index], ends])

    own_1 = begin(own)
    own_2 = forward(*own_1)
    left_1 = begin(left)
    right_1 = begin(right)
    mine = gather(own, *own_1, *own_2, 0)
    total = gram_add(core, mine, swap(mine), None)
    left_1 = after(left_1, [total])
    right_1 = after(right_1, [total])
    (far,) = after([far], [total])
    left_2 = forward(*left_1)
    right_2 = forward(*right_1)
    far_1 = begin(far)
    mine = gather(left, *left_1, *left_2, 0)
    theirs = swap(mine)
    right, *sides = after([right, *right_1, *right_2], [mine])
    mine_r = gather(right, *sides, 0)
    theirs_r = swap(mine_r)
    total = gram_add(core, mine, theirs, total)
    far, *far_1 = after([far, *far_1], [total])
    far_2 = forward(*far_1)
    total = gram_add(core, mine_r, theirs_r, total, tile=512)
    far_2 = after(far_2, [total])
    return gram_add(core, *finish([far, *far_1], far_2), total, 1 / (rows * 128))


def solution(mesh):
    fine = Mesh(mesh.devices.reshape(2, 4, 2, 4, 2), AXES)

    return jax.shard_map(
        shards,
        mesh=fine,
        in_specs=(P(AXES, None),),
        out_specs=P(("xl", "z"), ("xh", "y", "core")),
        check_vma=False,
    )
```

time: 404 us -> 203 us (0.50)
  waiting for transfers between devices: 291 us -> 122 us
  matrix products: 59.7 us -> 0 us
  starting transfers between devices: 0.04 us -> 38.5 us
  Pallas kernels: 0 us -> 35.6 us
  blocking collectives: 25 us -> 0 us
  between operations: 13.4 us -> 0.31 us
  other arithmetic: 12.5 us -> 5.49 us
    psum x1 -> x0, waiting for transfers between devices: 201 us -> none  [broadcast(): return lax.psum(block, axis)]
    ppermute x0 -> x28, waiting for transfers between devices: none -> 122 us  [the longest x3 58.1 us: move_x(): return lax.ppermute(value, ('xl', 'xh'), pairs)]
    all_gather x1 -> x0, waiting for transfers between devices: 90.3 us -> none  [shards(): whole_columns = lax.all_gather(own_columns, 'row', axis=0, tiled=True)]
    dot_general x1 -> x0, matrix products: 59.7 us -> none  [shards(): lax.dot_general(row_panel, whole_columns, (((0,), (0,)), ((), ())), preci...]
    ppermute x0 -> x28, starting transfers between devices: none -> 38.5 us  [the longest x16 27.6 us: move_ring(): return lax.ppermute(value, ('z', 'y', 'core'), pairs)]
    pallas_call x0 -> x4, Pallas kernels: none -> 35.6 us  [gram_add(): pl.pallas_call(functools.partial(gram_kernel, scale=scale, tile=tile, las...]
    all_to_all x1 -> x0, blocking collectives: 25 us -> none  [shards(): lax.all_to_all(layer_inputs, 'col', split_axis=1, concat_axis=0, tiled=True)]
    select_n x1, other arithmetic: 12.5 us -> 1.36 us  [shards(): jnp.where(first, got, block)]
  transfers between devices with their start and end apart: 2 -> 28, of which waited for: 2 -> 16; matrix products, arithmetic and copies ran while one was open for 0% -> 1% of each run, Pallas kernels for 0% -> 13%
where the time goes in v1:
time: 203 us; the launch traced here: 202 us
  waiting for transfers between devices  122 us (60%)
  starting transfers between devices  38.5 us (19%)
  Pallas kernels  35.6 us (18%)
  other arithmetic  5.49 us (3%)
    ppermute x3, waiting for transfers between devices, move_x(): return lax.ppermute(value, ('xl', 'xh'), pairs)  58.1 us
    ppermute x16, waiting for transfers between devices, move_ring(): return lax.ppermute(value, ('z', 'y', 'core'), pairs)  46.7 us
    pallas_call x4, Pallas kernels, gram_add(): pl.pallas_call(functools.partial(gram_kernel, scale=scale, tile=tile, las...  35.6 us
    ppermute x16, starting transfers between devices, move_ring(): return lax.ppermute(value, ('z', 'y', 'core'), pairs)  27.6 us
    ppermute x3, waiting for transfers between devices, move(): return lax.ppermute(value, ('z', 'y', 'core'), pairs)  11.8 us
    ppermute x3, starting transfers between devices, move(): return lax.ppermute(value, ('z', 'y', 'core'), pairs)  5.55 us
    ppermute x6, waiting for transfers between devices, swap(): return lax.ppermute(value, 'core', [(0, 1), (1, 0)])  5.03 us
    ppermute x3, starting transfers between devices, move_x(): return lax.ppermute(value, ('xl', 'xh'), pairs)  5 us
  transfers between devices with their start and end apart: 28, of which 16 were waited for; matrix products, arithmetic and copies ran while one was open for 1% of the time, Pallas kernels for 13%

profile of v1, /device:TPU:0, one launch (start us, length us, event | category | flops | bytes accessed | tf_op | source)
XLA Modules:
  0.0 202.2 jit_solution(10391863120826245802)
XLA Ops:
  0.0 2.9 %collective-permute-done = f32[16,16384]{1,0:T(8,128)S(1)} collective-permute-done((f32[16,16384]{1,0:T(8,128)}, f32[16,16384]{1,0:T(8,128)S(1)}, u32[]{:S(2)}, u32[]{:S(2)}) %collective-permute-start) | collective-permute-done | bytes 1048608 | tf_op jit(solution)/shard_map/ppermute | solution.py:39
  2.9 1.4 broadcast_select_fusion
  4.4 1.8 collective-permute-start.1
  6.2 1.6 collective-permute-start.2
  7.9 2.2 %collective-permute-start.3 = (f32[2,32,2048]{2,1,0:T(8,128)S(1)}, f32[2,32,2048]{2,1,0:T(8,128)}, u32[]{:S(2)}, u32[]{:S(2)}) collective-permute-start(f32[2,32,2048]{2,1,0:T(8,128)S(1)} %pad_maximum_fusion.9), channel_id=1, source_target_pairs={{0,4},{1,33},{2,6},{3,35},{4,0},{5,37},{6,2},{7,39},{16,20},{17,49... | collective-permute-start | bytes 1572872 | tf_op jit(solution)/shard_map/ppermute | solution.py:20
  10.1 4.7 %collective-permute-done.1 = f32[2,32,2048]{2,1,0:T(8,128)S(1)} collective-permute-done((f32[2,32,2048]{2,1,0:T(8,128)S(1)}, f32[2,32,2048]{2,1,0:T(8,128)S(1)}, u32[]{:S(2)}, u32[]{:S(2)}) %collective-permute-start.1) | collective-permute-done | bytes 524320 | tf_op jit(solution)/shard_map/ppermute | solution.py:20
  14.9 0.6 collective-permute-done.2
  15.5 6.5 %collective-permute-done.3 = f32[2,32,2048]{2,1,0:T(8,128)} collective-permute-done((f32[2,32,2048]{2,1,0:T(8,128)S(1)}, f32[2,32,2048]{2,1,0:T(8,128)}, u32[]{:S(2)}, u32[]{:S(2)}) %collective-permute-start.3) | collective-permute-done | bytes 524320 | tf_op jit(solution)/shard_map/ppermute | solution.py:20
  22.0 1.2 pad_maximum_fusion.6
  23.2 0.3 constant_dynamic-slice_fusion
  23.6 2.0 collective-permute-start.7
  25.5 2.2 %collective-permute-start.8 = (f32[1,128,2048]{2,1,0:T(8,128)S(1)}, f32[1,128,2048]{2,1,0:T(8,128)S(1)}, u32[]{:S(2)}, u32[]{:S(2)}) collective-permute-start(f32[1,128,2048]{2,1,0:T(8,128)S(1)} %bitcast.45), channel_id=1, source_target_pairs={{0,48},{1,7},{2,50},{3,1},{4,52},{5,3},{6,54},{7,5},{16,0},{17,23}... | collective-permute-start | bytes 3145736 | tf_op jit(solution)/shard_map/ppermute | solution.py:29
  27.8 12.7 %collective-permute-done.7 = f32[1,128,2048]{2,1,0:T(8,128)S(1)} collective-permute-done((f32[1,128,2048]{2,1,0:T(8,128)S(1)}, f32[1,128,2048]{2,1,0:T(8,128)S(1)}, u32[]{:S(2)}, u32[]{:S(2)}) %collective-permute-start.7) | collective-permute-done | bytes 1048608 | tf_op jit(solution)/shard_map/ppermute | solution.py:29
  40.6 3.3 %collective-permute-start.10 = (f32[1,64,2048]{2,1,0:T(8,128)S(1)}, f32[1,64,2048]{2,1,0:T(8,128)S(1)}, u32[]{:S(2)}, u32[]{:S(2)}) collective-permute-start(f32[1,64,2048]{2,1,0:T(8,128)S(1)} %slice.33), channel_id=1, source_target_pairs={{0,48},{1,7},{2,50},{3,1},{4,52},{5,3},{6,54},{7,5},{16,0},{17,23}... | collective-permute-start | bytes 1572872 | tf_op jit(solution)/shard_map/ppermute | solution.py:29
  43.9 7.0 %collective-permute-done.9 = f32[1,64,2048]{2,1,0:T(8,128)S(1)} collective-permute-done((f32[1,64,2048]{2,1,0:T(8,128)S(1)}, f32[1,64,2048]{2,1,0:T(8,128)S(1)}, u32[]{:S(2)}, u32[]{:S(2)}) %collective-permute-start.9) | collective-permute-done | bytes 524320 | tf_op jit(solution)/shard_map/ppermute | solution.py:29
  51.4 1.6 collective-permute-start.4
  53.0 25.2 %collective-permute-done.4 = f32[4,32,2048]{2,1,0:T(8,128)S(1)} collective-permute-done((f32[4,32,2048]{2,1,0:T(8,128)S(1)}, f32[4,32,2048]{2,1,0:T(8,128)S(1)}, u32[]{:S(2)}, u32[]{:S(2)}) %collective-permute-start.4) | collective-permute-done | bytes 1048608 | tf_op jit(solution)/shard_map/ppermute | solution.py:35
  78.2 0.7 collective-permute-start.14
  78.9 2.6 %collective-permute-start.15 = (f32[1,128,2048]{2,1,0:T(8,128)S(1)}, f32[1,128,2048]{2,1,0:T(8,128)S(1)}, u32[]{:S(2)}, u32[]{:S(2)}) collective-permute-start(f32[1,128,2048]{2,1,0:T(8,128)S(1)} %bitcast.55), channel_id=1, source_target_pairs={{0,48},{1,7},{2,50},{3,1},{4,52},{5,3},{6,54},{7,5},{16,0},{17,23}... | collective-permute-start | bytes 3145736 | tf_op jit(solution)/shard_map/ppermute | solution.py:29
  81.5 1.5 collective-permute-start.5
  83.1 8.7 %shard_map.17.refs_2_ = f32[2048,1024]{1,0:T(8,128)S(1)} custom-call(s32[1]{0:T(128)} %bitcast.core_ref, f32[4,128,2048]{2,1,0:T(8,128)S(1)} %pad_maximum_fusion.refs_0_, f32[4,128,2048]{2,1,0:T(8,128)S(1)} %collective-permute-done.11.refs_1_), custom_call_target="tpu_custom_call" | custom-call | flops 6442450944 | bytes 16777216 | tf_op jit(solution)/shard_map/pallas_call | solution.py:98
  91.8 2.5 %collective-permute-done.14 = f32[1,128,2048]{2,1,0:T(8,128)S(1)} collective-permute-done((f32[1,128,2048]{2,1,0:T(8,128)S(1)}, f32[1,128,2048]{2,1,0:T(8,128)S(1)}, u32[]{:S(2)}, u32[]{:S(2)}) %collective-permute-start.14) | collective-permute-done | bytes 1048608 | tf_op jit(solution)/shard_map/ppermute | solution.py:29
  94.4 1.5 collective-permute-start.16
  95.9 1.9 collective-permute-start.17
  97.8 7.7 %collective-permute-done.5 = f32[4,32,2048]{2,1,0:T(8,128)S(1)} collective-permute-done((f32[4,32,2048]{2,1,0:T(8,128)S(1)}, f32[4,32,2048]{2,1,0:T(8,128)S(1)}, u32[]{:S(2)}, u32[]{:S(2)}) %collective-permute-start.5) | collective-permute-done | bytes 1048608 | tf_op jit(solution)/shard_map/ppermute | solution.py:35
  105.5 0.7 collective-permute-start.21
  106.2 2.6 %collective-permute-start.22 = (f32[1,128,2048]{2,1,0:T(8,128)S(1)}, f32[1,128,2048]{2,1,0:T(8,128)S(1)}, u32[]{:S(2)}, u32[]{:S(2)}) collective-permute-start(f32[1,128,2048]{2,1,0:T(8,128)S(1)} %bitcast.52), channel_id=1, source_target_pairs={{0,48},{1,7},{2,50},{3,1},{4,52},{5,3},{6,54},{7,5},{16,0},{17,23}... | collective-permute-start | bytes 3145736 | tf_op jit(solution)/shard_map/ppermute | solution.py:29
  109.0 0.4 pad_maximum_fusion.1.refs_0_
  109.5 12.1 %collective-permute-done.21 = f32[1,128,2048]{2,1,0:T(8,128)S(1)} collective-permute-done((f32[1,128,2048]{2,1,0:T(8,128)S(1)}, f32[1,128,2048]{2,1,0:T(8,128)S(1)}, u32[]{:S(2)}, u32[]{:S(2)}) %collective-permute-start.21) | collective-permute-done | bytes 1048608 | tf_op jit(solution)/shard_map/ppermute | solution.py:29
  121.7 1.5 collective-permute-start.23
  123.2 1.9 collective-permute-start.24
  125.1 7.0 %collective-permute-done.23 = f32[1,64,2048]{2,1,0:T(8,128)S(1)} collective-permute-done((f32[1,64,2048]{2,1,0:T(8,128)S(1)}, f32[1,64,2048]{2,1,0:T(8,128)S(1)}, u32[]{:S(2)}, u32[]{:S(2)}) %collective-permute-start.23) | collective-permute-done | bytes 524320 | tf_op jit(solution)/shard_map/ppermute | solution.py:29
  132.5 0.4 pad_maximum_fusion.2.refs_0_
  133.0 1.9 collective-permute-start.6
  134.9 25.2 %collective-permute-done.6 = f32[4,32,2048]{2,1,0:T(8,128)S(1)} collective-permute-done((f32[4,32,2048]{2,1,0:T(8,128)S(1)}, f32[4,32,2048]{2,1,0:T(8,128)S(1)}, u32[]{:S(2)}, u32[]{:S(2)}) %collective-permute-start.6) | collective-permute-done | bytes 1048608 | tf_op jit(solution)/shard_map/ppermute | solution.py:35
  160.1 2.0 collective-permute-start.12
  162.1 1.2 collective-permute-start.13
  163.3 8.7 %shard_map.18.refs_2_ = f32[2048,1024]{1,0:T(8,128)S(1)} custom-call(s32[1]{0:T(128)} %bitcast.core_ref, f32[4,128,2048]{2,1,0:T(8,128)S(1)} %pad_maximum_fusion.1.refs_0_, f32[4,128,2048]{2,1,0:T(8,128)S(1)} %collective-permute-done.18.refs_1_, f32[2048,1024]{1,0:T(8,128)S(1)} %shard_map.17.refs_2_), custom_call_target="tpu_custom_call", output_to_operand_aliasing={{}: (3, {})} | custom-call | flops 6442450944 | bytes 16777216 | tf_op jit(solution)/shard_map/pallas_call | solution.py:98
  172.0 4.1 %collective-permute-done.12 = f32[1,128,2048]{2,1,0:T(8,128)S(1)} collective-permute-done((f32[1,128,2048]{2,1,0:T(8,128)S(1)}, f32[1,128,2048]{2,1,0:T(8,128)S(1)}, u32[]{:S(2)}, u32[]{:S(2)}) %collective-permute-start.12) | collective-permute-done | bytes 1048608 | tf_op jit(solution)/shard_map/ppermute | solution.py:29
  176.1 0.8 collective-permute-done.13
  176.9 0.3 pad_maximum_fusion.5
  177.4 1.3 collective-permute-start.19
  178.7 2.0 %collective-permute-start.20 = (f32[1,64,2048]{2,1,0:T(8,128)S(1)}, f32[1,64,2048]{2,1,0:T(8,128)S(1)}, u32[]{:S(2)}, u32[]{:S(2)}) collective-permute-start(f32[1,64,2048]{2,1,0:T(8,128)S(1)} %slice.29), channel_id=1, source_target_pairs={{0,48},{1,7},{2,50},{3,1},{4,52},{5,3},{6,54},{7,5},{16,0},{17,23}... | collective-permute-start | bytes 1572872 | tf_op jit(solution)/shard_map/ppermute | solution.py:29
  180.7 8.5 %shard_map.19.refs_2_ = f32[2048,1024]{1,0:T(8,128)S(1)} custom-call(s32[1]{0:T(128)} %bitcast.core_ref, f32[4,128,2048]{2,1,0:T(8,128)S(1)} %pad_maximum_fusion.2.refs_0_, f32[4,128,2048]{2,1,0:T(8,128)S(1)} %collective-permute-done.25.refs_1_, f32[2048,1024]{1,0:T(8,128)S(1)} %shard_map.18.refs_2_), custom_call_target="tpu_custom_call", output_to_operand_aliasing={{}: (3, {})} | custom-call | flops 6442450944 | bytes 16777216 | tf_op jit(solution)/shard_map/pallas_call | solution.py:98
  189.4 0.5 pad_maximum_fusion.3.refs_0_
  189.9 2.2 %collective-permute-done.27 = f32[1,128,2048]{2,1,0:T(8,128)S(1)} collective-permute-done((f32[1,128,2048]{2,1,0:T(8,128)S(1)}, f32[1,128,2048]{2,1,0:T(8,128)S(1)}, u32[]{:S(2)}, u32[]{:S(2)}) %collective-permute-start.27) | collective-permute-done | bytes 1048608 | tf_op jit(solution)/shard_map/ppermute | solution.py:39
  192.1 0.4 pad_maximum_fusion.4.refs_1_
  192.5 9.7 %shard_map.20 = f32[2048,1024]{1,0:T(8,128)} custom-call(s32[1]{0:T(128)} %bitcast.core_ref, f32[4,128,2048]{2,1,0:T(8,128)S(1)} %pad_maximum_fusion.3.refs_0_, f32[4,128,2048]{2,1,0:T(8,128)S(1)} %pad_maximum_fusion.4.refs_1_, f32[2048,1024]{1,0:T(8,128)S(1)} %shard_map.19.refs_2_), custom_call_target="tpu_custom_call" | custom-call | flops 6442450944 | bytes 16777216 | tf_op jit(solution)/shard_map/pallas_call | solution.py:98
  (40 shorter events, 2.1 us)
Async XLA Ops:
  0.0 2.9 %collective-permute-start = (f32[16,16384]{1,0:T(8,128)}, f32[16,16384]{1,0:T(8,128)S(1)}, u32[]{:S(2)}, u32[]{:S(2)}) collective-permute-start(f32[16,16384]{1,0:T(8,128)} %param.1), channel_id=1, source_target_pairs={{0,1},{1,0},{2,3},{3,2},{4,5},{5,4},{6,7},{7,6},{8,9},{9,8},{10,11... | collective-permute-start | bytes 3145736 | tf_op jit(solution)/shard_map/ppermute | solution.py:39
  4.4 10.5 %collective-permute-start.1 = (f32[2,32,2048]{2,1,0:T(8,128)S(1)}, f32[2,32,2048]{2,1,0:T(8,128)S(1)}, u32[]{:S(2)}, u32[]{:S(2)}) collective-permute-start(f32[2,32,2048]{2,1,0:T(8,128)S(1)} %pad_maximum_fusion.7), channel_id=1, source_target_pairs={{0,2},{1,17},{2,4},{3,19},{4,6},{5,21},{6,0},{7,23},{16,18},{17,33... | collective-permute-start | bytes 1572872 | tf_op jit(solution)/shard_map/ppermute | solution.py:20
  6.2 9.2 %collective-permute-start.2 = (f32[2,32,2048]{2,1,0:T(8,128)S(1)}, f32[2,32,2048]{2,1,0:T(8,128)S(1)}, u32[]{:S(2)}, u32[]{:S(2)}) collective-permute-start(f32[2,32,2048]{2,1,0:T(8,128)S(1)} %pad_maximum_fusion.8), channel_id=1, source_target_pairs={{0,6},{1,49},{2,0},{3,51},{4,2},{5,53},{6,4},{7,55},{16,22},{17,1}... | collective-permute-start | bytes 1572872 | tf_op jit(solution)/shard_map/ppermute | solution.py:20
  7.9 14.0 %collective-permute-start.3 = (f32[2,32,2048]{2,1,0:T(8,128)S(1)}, f32[2,32,2048]{2,1,0:T(8,128)}, u32[]{:S(2)}, u32[]{:S(2)}) collective-permute-start(f32[2,32,2048]{2,1,0:T(8,128)S(1)} %pad_maximum_fusion.9), channel_id=1, source_target_pairs={{0,4},{1,33},{2,6},{3,35},{4,0},{5,37},{6,2},{7,39},{16,20},{17,49... | collective-permute-start | bytes 1572872 | tf_op jit(solution)/shard_map/ppermute | solution.py:20
  23.6 16.9 %collective-permute-start.7 = (f32[1,128,2048]{2,1,0:T(8,128)S(1)}, f32[1,128,2048]{2,1,0:T(8,128)S(1)}, u32[]{:S(2)}, u32[]{:S(2)}) collective-permute-start(f32[1,128,2048]{2,1,0:T(8,128)S(1)} %bitcast.44), channel_id=1, source_target_pairs={{0,16},{1,3},{2,18},{3,5},{4,20},{5,7},{6,22},{7,1},{16,32},{17,19... | collective-permute-start | bytes 3145736 | tf_op jit(solution)/shard_map/ppermute | solution.py:29
  25.5 15.0 %collective-permute-start.8 = (f32[1,128,2048]{2,1,0:T(8,128)S(1)}, f32[1,128,2048]{2,1,0:T(8,128)S(1)}, u32[]{:S(2)}, u32[]{:S(2)}) collective-permute-start(f32[1,128,2048]{2,1,0:T(8,128)S(1)} %bitcast.45), channel_id=1, source_target_pairs={{0,48},{1,7},{2,50},{3,1},{4,52},{5,3},{6,54},{7,5},{16,0},{17,23}... | collective-permute-start | bytes 3145736 | tf_op jit(solution)/shard_map/ppermute | solution.py:29
  40.5 10.5 %collective-permute-start.9 = (f32[1,64,2048]{2,1,0:T(8,128)S(1)}, f32[1,64,2048]{2,1,0:T(8,128)S(1)}, u32[]{:S(2)}, u32[]{:S(2)}) collective-permute-start(f32[1,64,2048]{2,1,0:T(8,128)S(1)} %slice.32), channel_id=1, source_target_pairs={{0,16},{1,3},{2,18},{3,5},{4,20},{5,7},{6,22},{7,1},{16,32},{17,19... | collective-permute-start | bytes 1572872 | tf_op jit(solution)/shard_map/ppermute | solution.py:29
  40.6 10.3 %collective-permute-start.10 = (f32[1,64,2048]{2,1,0:T(8,128)S(1)}, f32[1,64,2048]{2,1,0:T(8,128)S(1)}, u32[]{:S(2)}, u32[]{:S(2)}) collective-permute-start(f32[1,64,2048]{2,1,0:T(8,128)S(1)} %slice.33), channel_id=1, source_target_pairs={{0,48},{1,7},{2,50},{3,1},{4,52},{5,3},{6,54},{7,5},{16,0},{17,23}... | collective-permute-start | bytes 1572872 | tf_op jit(solution)/shard_map/ppermute | solution.py:29
  51.3 31.8 %collective-permute-start.11 = (f32[4,128,2048]{2,1,0:T(8,128)S(1)}, f32[4,128,2048]{2,1,0:T(8,128)S(1)}, u32[]{:S(2)}, u32[]{:S(2)}) collective-permute-start(f32[4,128,2048]{2,1,0:T(8,128)S(1)} %pad_maximum_fusion.refs_0_), channel_id=1, source_target_pairs={{0,1},{1,0},{2,3},{3,2},{4,5},{5,4},{6,7},{7,6},{8,9},{9,8},{10,11... | collective-permute-start | bytes 12582920 | tf_op jit(solution)/shard_map/ppermute | solution.py:39
  51.4 26.8 %collective-permute-start.4 = (f32[4,32,2048]{2,1,0:T(8,128)S(1)}, f32[4,32,2048]{2,1,0:T(8,128)S(1)}, u32[]{:S(2)}, u32[]{:S(2)}) collective-permute-start(f32[4,32,2048]{2,1,0:T(8,128)S(1)} %get-tuple-element.39), channel_id=1, source_target_pairs={{0,64},{64,8},{8,72},{72,0},{1,65},{65,9},{9,73},{73,1},{2,66},{66... | collective-permute-start | bytes 3145736 | tf_op jit(solution)/shard_map/ppermute | solution.py:35
  78.2 16.1 %collective-permute-start.14 = (f32[1,128,2048]{2,1,0:T(8,128)S(1)}, f32[1,128,2048]{2,1,0:T(8,128)S(1)}, u32[]{:S(2)}, u32[]{:S(2)}) collective-permute-start(f32[1,128,2048]{2,1,0:T(8,128)S(1)} %bitcast.54), channel_id=1, source_target_pairs={{0,16},{1,3},{2,18},{3,5},{4,20},{5,7},{6,22},{7,1},{16,32},{17,19... | collective-permute-start | bytes 3145736 | tf_op jit(solution)/shard_map/ppermute | solution.py:29
  78.9 15.4 %collective-permute-start.15 = (f32[1,128,2048]{2,1,0:T(8,128)S(1)}, f32[1,128,2048]{2,1,0:T(8,128)S(1)}, u32[]{:S(2)}, u32[]{:S(2)}) collective-permute-start(f32[1,128,2048]{2,1,0:T(8,128)S(1)} %bitcast.55), channel_id=1, source_target_pairs={{0,48},{1,7},{2,50},{3,1},{4,52},{5,3},{6,54},{7,5},{16,0},{17,23}... | collective-permute-start | bytes 3145736 | tf_op jit(solution)/shard_map/ppermute | solution.py:29
  81.5 24.0 %collective-permute-start.5 = (f32[4,32,2048]{2,1,0:T(8,128)S(1)}, f32[4,32,2048]{2,1,0:T(8,128)S(1)}, u32[]{:S(2)}, u32[]{:S(2)}) collective-permute-start(f32[4,32,2048]{2,1,0:T(8,128)S(1)} %get-tuple-element.38), channel_id=1, source_target_pairs={{0,72},{64,0},{8,64},{72,8},{1,73},{65,1},{9,65},{73,9},{2,74},{66... | collective-permute-start | bytes 3145736 | tf_op jit(solution)/shard_map/ppermute | solution.py:35
  94.4 14.5 %collective-permute-start.16 = (f32[1,64,2048]{2,1,0:T(8,128)S(1)}, f32[1,64,2048]{2,1,0:T(8,128)S(1)}, u32[]{:S(2)}, u32[]{:S(2)}) collective-permute-start(f32[1,64,2048]{2,1,0:T(8,128)S(1)} %slice.26), channel_id=1, source_target_pairs={{0,16},{1,3},{2,18},{3,5},{4,20},{5,7},{6,22},{7,1},{16,32},{17,19... | collective-permute-start | bytes 1572872 | tf_op jit(solution)/shard_map/ppermute | solution.py:29
  95.9 13.0 %collective-permute-start.17 = (f32[1,64,2048]{2,1,0:T(8,128)S(1)}, f32[1,64,2048]{2,1,0:T(8,128)S(1)}, u32[]{:S(2)}, u32[]{:S(2)}) collective-permute-start(f32[1,64,2048]{2,1,0:T(8,128)S(1)} %slice.27), channel_id=1, source_target_pairs={{0,48},{1,7},{2,50},{3,1},{4,52},{5,3},{6,54},{7,5},{16,0},{17,23}... | collective-permute-start | bytes 1572872 | tf_op jit(solution)/shard_map/ppermute | solution.py:29
  105.5 16.1 %collective-permute-start.21 = (f32[1,128,2048]{2,1,0:T(8,128)S(1)}, f32[1,128,2048]{2,1,0:T(8,128)S(1)}, u32[]{:S(2)}, u32[]{:S(2)}) collective-permute-start(f32[1,128,2048]{2,1,0:T(8,128)S(1)} %bitcast.51), channel_id=1, source_target_pairs={{0,16},{1,3},{2,18},{3,5},{4,20},{5,7},{6,22},{7,1},{16,32},{17,19... | collective-permute-start | bytes 3145736 | tf_op jit(solution)/shard_map/ppermute | solution.py:29
  106.2 15.4 %collective-permute-start.22 = (f32[1,128,2048]{2,1,0:T(8,128)S(1)}, f32[1,128,2048]{2,1,0:T(8,128)S(1)}, u32[]{:S(2)}, u32[]{:S(2)}) collective-permute-start(f32[1,128,2048]{2,1,0:T(8,128)S(1)} %bitcast.52), channel_id=1, source_target_pairs={{0,48},{1,7},{2,50},{3,1},{4,52},{5,3},{6,54},{7,5},{16,0},{17,23}... | collective-permute-start | bytes 3145736 | tf_op jit(solution)/shard_map/ppermute | solution.py:29
  109.4 53.9 %collective-permute-start.18 = (f32[4,128,2048]{2,1,0:T(8,128)S(1)}, f32[4,128,2048]{2,1,0:T(8,128)S(1)}, u32[]{:S(2)}, u32[]{:S(2)}) collective-permute-start(f32[4,128,2048]{2,1,0:T(8,128)S(1)} %pad_maximum_fusion.1.refs_0_), channel_id=1, source_target_pairs={{0,1},{1,0},{2,3},{3,2},{4,5},{5,4},{6,7},{7,6},{8,9},{9,8},{10,11... | collective-permute-start | bytes 12582920 | tf_op jit(solution)/shard_map/ppermute | solution.py:39
  121.7 10.5 %collective-permute-start.23 = (f32[1,64,2048]{2,1,0:T(8,128)S(1)}, f32[1,64,2048]{2,1,0:T(8,128)S(1)}, u32[]{:S(2)}, u32[]{:S(2)}) collective-permute-start(f32[1,64,2048]{2,1,0:T(8,128)S(1)} %slice.30), channel_id=1, source_target_pairs={{0,16},{1,3},{2,18},{3,5},{4,20},{5,7},{6,22},{7,1},{16,32},{17,19... | collective-permute-start | bytes 1572872 | tf_op jit(solution)/shard_map/ppermute | solution.py:29
  123.2 9.3 %collective-permute-start.24 = (f32[1,64,2048]{2,1,0:T(8,128)S(1)}, f32[1,64,2048]{2,1,0:T(8,128)S(1)}, u32[]{:S(2)}, u32[]{:S(2)}) collective-permute-start(f32[1,64,2048]{2,1,0:T(8,128)S(1)} %slice.31), channel_id=1, source_target_pairs={{0,48},{1,7},{2,50},{3,1},{4,52},{5,3},{6,54},{7,5},{16,0},{17,23}... | collective-permute-start | bytes 1572872 | tf_op jit(solution)/shard_map/ppermute | solution.py:29
  132.9 47.8 %collective-permute-start.25 = (f32[4,128,2048]{2,1,0:T(8,128)S(1)}, f32[4,128,2048]{2,1,0:T(8,128)S(1)}, u32[]{:S(2)}, u32[]{:S(2)}) collective-permute-start(f32[4,128,2048]{2,1,0:T(8,128)S(1)} %pad_maximum_fusion.2.refs_0_), channel_id=1, source_target_pairs={{0,1},{1,0},{2,3},{3,2},{4,5},{5,4},{6,7},{7,6},{8,9},{9,8},{10,11... | collective-permute-start | bytes 12582920 | tf_op jit(solution)/shard_map/ppermute | solution.py:39
  133.0 27.1 %collective-permute-start.6 = (f32[4,32,2048]{2,1,0:T(8,128)S(1)}, f32[4,32,2048]{2,1,0:T(8,128)S(1)}, u32[]{:S(2)}, u32[]{:S(2)}) collective-permute-start(f32[4,32,2048]{2,1,0:T(8,128)S(1)} %get-tuple-element.21), channel_id=1, source_target_pairs={{0,8},{64,72},{8,0},{72,64},{1,9},{65,73},{9,1},{73,65},{2,10},{66... | collective-permute-start | bytes 3145736 | tf_op jit(solution)/shard_map/ppermute | solution.py:35
  160.1 16.0 %collective-permute-start.12 = (f32[1,128,2048]{2,1,0:T(8,128)S(1)}, f32[1,128,2048]{2,1,0:T(8,128)S(1)}, u32[]{:S(2)}, u32[]{:S(2)}) collective-permute-start(f32[1,128,2048]{2,1,0:T(8,128)S(1)} %bitcast.47), channel_id=1, source_target_pairs={{0,16},{1,3},{2,18},{3,5},{4,20},{5,7},{6,22},{7,1},{16,32},{17,19... | collective-permute-start | bytes 3145736 | tf_op jit(solution)/shard_map/ppermute | solution.py:29
  162.1 14.8 %collective-permute-start.13 = (f32[1,128,2048]{2,1,0:T(8,128)S(1)}, f32[1,128,2048]{2,1,0:T(8,128)S(1)}, u32[]{:S(2)}, u32[]{:S(2)}) collective-permute-start(f32[1,128,2048]{2,1,0:T(8,128)S(1)} %bitcast.48), channel_id=1, source_target_pairs={{0,48},{1,7},{2,50},{3,1},{4,52},{5,3},{6,54},{7,5},{16,0},{17,23}... | collective-permute-start | bytes 3145736 | tf_op jit(solution)/shard_map/ppermute | solution.py:29
  177.2 14.8 %collective-permute-start.26 = (f32[3,128,2048]{2,1,0:T(8,128)S(1)}, f32[3,128,2048]{2,1,0:T(8,128)S(1)}, u32[]{:S(2)}, u32[]{:S(2)}) collective-permute-start(f32[3,128,2048]{2,1,0:T(8,128)S(1)} %pad_maximum_fusion.5), channel_id=1, source_target_pairs={{0,1},{1,0},{2,3},{3,2},{4,5},{5,4},{6,7},{7,6},{8,9},{9,8},{10,11... | collective-permute-start | bytes 9437192 | tf_op jit(solution)/shard_map/ppermute | solution.py:39
  177.4 11.8 %collective-permute-start.19 = (f32[1,64,2048]{2,1,0:T(8,128)S(1)}, f32[1,64,2048]{2,1,0:T(8,128)S(1)}, u32[]{:S(2)}, u32[]{:S(2)}) collective-permute-start(f32[1,64,2048]{2,1,0:T(8,128)S(1)} %slice.28), channel_id=1, source_target_pairs={{0,16},{1,3},{2,18},{3,5},{4,20},{5,7},{6,22},{7,1},{16,32},{17,19... | collective-permute-start | bytes 1572872 | tf_op jit(solution)/shard_map/ppermute | solution.py:29
  178.7 10.5 %collective-permute-start.20 = (f32[1,64,2048]{2,1,0:T(8,128)S(1)}, f32[1,64,2048]{2,1,0:T(8,128)S(1)}, u32[]{:S(2)}, u32[]{:S(2)}) collective-permute-start(f32[1,64,2048]{2,1,0:T(8,128)S(1)} %slice.29), channel_id=1, source_target_pairs={{0,48},{1,7},{2,50},{3,1},{4,52},{5,3},{6,54},{7,5},{16,0},{17,23}... | collective-permute-start | bytes 1572872 | tf_op jit(solution)/shard_map/ppermute | solution.py:29
  189.3 2.7 %collective-permute-start.27 = (f32[1,128,2048]{2,1,0:T(8,128)S(1)}, f32[1,128,2048]{2,1,0:T(8,128)S(1)}, u32[]{:S(2)}, u32[]{:S(2)}) collective-permute-start(f32[1,128,2048]{2,1,0:T(8,128)S(1)} %constant_dynamic-update-slice_fusion), channel_id=1, source_target_pairs={{0,1},{1,0},{2,3},{3,2},{4,5},{5,4},{6,7},{7,6},{8,9},{9,8},{10,11... | collective-permute-start | bytes 3145736 | tf_op jit(solution)/shard_map/ppermute | solution.py:39

commit v2 on v1

--- a/solution.py
+++ b/solution.py
@@ -54,19 +54,22 @@
 
 
 def gram_kernel(core_ref, *refs, scale, tile, last):
-    mine, theirs = refs[:2]
-    total = refs[2] if len(refs) == 5 else None
+    mine, theirs = refs[:2], refs[2:4]
+    total = refs[4] if len(refs) == 7 else None
     out, right = refs[-2:]
     first = core_ref[0] == 0
-    outer, inner, cols = mine.shape
+    inner, cols = mine[0].shape[1:]
+    lengths = [part.shape[0] for part in mine]
+    outer = sum(lengths)
     width, piece, count = cols // 2, inner // outer, outer * inner
+    where = [(k, i) for k, length in enumerate(lengths) for i in range(length)]
 
     @pl.when(pl.program_id(0) == 0)
     def _():
-        for i in range(outer):
+        for i, (k, n) in enumerate(where):
             for j in range(outer):
                 rows = pl.ds(j * piece, piece)
-                ours, other = mine[i, rows, :width], theirs[i, rows, width:]
+                ours, other = mine[k][n, rows, :width], theirs[k][n, rows, width:]
                 high, low = split(jnp.where(first, ours, other))
                 at = (j * outer + i) * piece
                 right[pl.ds(at, piece), :] = high
@@ -74,7 +77,12 @@
                 right[pl.ds(2 * count + at, piece), :] = high
 
     at = pl.ds(pl.multiple_of(pl.program_id(0) * tile, tile), tile)
-    left = jnp.where(first, theirs[:, :, at], mine[:, :, at]).reshape(count, tile).T
+    left = jnp.concatenate(
+        [
+            jnp.where(first, theirs[k][:, :, at], mine[k][:, :, at]).reshape(-1, tile)
+            for k in range(len(mine))
+        ]
+    ).T
     high, low = split(left)
     part = jnp.dot(
         jnp.concatenate([high, high, low], axis=1),
@@ -90,10 +98,10 @@
 
 
 def gram_add(core, mine, theirs, total, scale=None, tile=256):
-    outer, inner, cols = mine.shape
+    outer, (inner, cols) = sum(m.shape[0] for m in mine), mine[0].shape[1:]
     width, count = cols // 2, outer * inner
     whole = pl.BlockSpec(memory_space=pltpu.VMEM)
-    args = [mine, theirs] + ([] if total is None else [total])
+    args = [*mine, *theirs] + ([] if total is None else [total])
     last = scale is not None
     return pl.pallas_call(
         functools.partial(gram_kernel, scale=scale, tile=tile, last=last),
@@ -105,8 +113,8 @@
             out_specs=pl.BlockSpec((tile, width), lambda m, c: (m, 0)) if last else whole,
             scratch_shapes=[pltpu.VMEM((3 * count, width), jnp.bfloat16)],
         ),
-        input_output_aliases={} if last or total is None else {3: 0},
-        compiler_params=pltpu.CompilerParams(vmem_limit_bytes=30 << 20),
+        input_output_aliases={} if last or total is None else {5: 0},
+        compiler_params=pltpu.CompilerParams(vmem_limit_bytes=12 << 20),
         cost_estimate=pl.CostEstimate(
             flops=6 * count * cols * width, bytes_accessed=16 << 20, transcendentals=0
         ),
@@ -140,9 +148,15 @@
 
     tokens = 8 * rows
     own = message(0).reshape(1, tokens, cols)
-    left = move_x(message(1), 1).reshape(1, tokens, cols)
-    right = move_x(message(3), 3).reshape(1, tokens, cols)
-    (second,) = after([message(2)], [left, right])
+    plus, minus = message(1), message(3)
+
+    def sides(part):
+        got = [move_x(plus[:, part], 1), move_x(minus[:, part], 3)]
+        return jnp.concatenate(got, axis=1).reshape(1, tokens, cols)
+
+    left = sides(slice(0, rows))
+    right = sides(slice(rows, 2 * rows))
+    (second,) = after([message(2)], [right])
     far = move_x(second, 2).reshape(1, tokens, cols)
 
     def begin(value):
@@ -155,36 +169,25 @@
         return far_a, far_b
 
     def finish(near, ends):
-        near = jnp.concatenate(near)
-        ends = jnp.concatenate(ends, axis=1)
-        theirs = jnp.concatenate([swap(near), swap(ends)])
-        return jnp.concatenate([near, ends]), theirs
-
-    def gather(value, ahead, back, far_a, far_b, index):
-        ends = jnp.concatenate([far_a[index], far_b[index]])
-        return jnp.stack([value[index], ahead[index], back[index], ends])
+        mine = (jnp.concatenate(near), jnp.concatenate(ends, axis=1))
+        return mine, (swap(mine[0]), swap(mine[1]))
 
     own_1 = begin(own)
     own_2 = forward(*own_1)
     left_1 = begin(left)
     right_1 = begin(right)
-    mine = gather(own, *own_1, *own_2, 0)
-    total = gram_add(core, mine, swap(mine), None)
+    total = gram_add(core, *finish([own, *own_1], own_2), None)
     left_1 = after(left_1, [total])
-    right_1 = after(right_1, [total])
-    (far,) = after([far], [total])
     left_2 = forward(*left_1)
+    right_1 = after(right_1, left_1)
     right_2 = forward(*right_1)
+    (far,) = after([far], right_1)
     far_1 = begin(far)
-    mine = gather(left, *left_1, *left_2, 0)
-    theirs = swap(mine)
-    right, *sides = after([right, *right_1, *right_2], [mine])
-    mine_r = gather(right, *sides, 0)
-    theirs_r = swap(mine_r)
-    total = gram_add(core, mine, theirs, total)
-    far, *far_1 = after([far, *far_1], [total])
+    total = gram_add(core, *finish([left, *left_1], left_2), total)
+    right_2 = after(right_2, [total])
+    far_1 = after(far_1, [total])
     far_2 = forward(*far_1)
-    total = gram_add(core, mine_r, theirs_r, total, tile=512)
+    total = gram_add(core, *finish([right, *right_1], right_2), total)
     far_2 = after(far_2, [total])
     return gram_add(core, *finish([far, *far_1], far_2), total, 1 / (rows * 128))
 

time: 203 us -> 173 us (0.85)
  waiting for transfers between devices: 122 us -> 87.5 us
  starting transfers between devices: 38.5 us -> 42.4 us
    ppermute x3 -> x5, waiting for transfers between devices: 58.1 us -> 23.3 us  [move_x(): return lax.ppermute(value, ('xl', 'xh'), pairs)]
    ppermute x3 -> x5, starting transfers between devices: 5 us -> 7.66 us  [move_x(): return lax.ppermute(value, ('xl', 'xh'), pairs)]
    ppermute x6 -> x9, waiting for transfers between devices: 5.03 us -> 5.53 us  [swap(): return lax.ppermute(value, 'core', [(0, 1), (1, 0)])]
  transfers between devices with their start and end apart: 28 -> 33, of which waited for: 16 -> 17; matrix products, arithmetic and copies ran while one was open for 1% -> 1% of each run, Pallas kernels for 13% -> 15%
where the time goes in v2:
time: 173 us; the launch traced here: 172 us
  waiting for transfers between devices  87.5 us (51%)
  starting transfers between devices  42.4 us (25%)
  Pallas kernels  36.2 us (21%)
  other arithmetic  4.05 us (2%)
    ppermute x16, waiting for transfers between devices, move_ring(): return lax.ppermute(value, ('z', 'y', 'core'), pairs)  46.9 us
    pallas_call x4, Pallas kernels, gram_add(): pl.pallas_call(functools.partial(gram_kernel, scale=scale, tile=tile, las...  36.2 us
    ppermute x16, starting transfers between devices, move_ring(): return lax.ppermute(value, ('z', 'y', 'core'), pairs)  27.6 us
    ppermute x5, waiting for transfers between devices, move_x(): return lax.ppermute(value, ('xl', 'xh'), pairs)  23.3 us
    ppermute x3, waiting for transfers between devices, move(): return lax.ppermute(value, ('z', 'y', 'core'), pairs)  11.8 us
    ppermute x5, starting transfers between devices, move_x(): return lax.ppermute(value, ('xl', 'xh'), pairs)  7.66 us
    ppermute x3, starting transfers between devices, move(): return lax.ppermute(value, ('z', 'y', 'core'), pairs)  5.55 us
    ppermute x9, waiting for transfers between devices, swap(): return lax.ppermute(value, 'core', [(0, 1), (1, 0)])  5.53 us
  transfers between devices with their start and end apart: 33, of which 17 were waited for; matrix products, arithmetic and copies ran while one was open for 1% of the time, Pallas kernels for 15%

profile of v2, /device:TPU:0, one launch (start us, length us, event | category | flops | bytes accessed | tf_op | source)
XLA Modules:
  0.0 171.9 jit_solution(8956420692627518725)
XLA Ops:
  0.0 2.9 %collective-permute-done = f32[16,16384]{1,0:T(8,128)S(1)} collective-permute-done((f32[16,16384]{1,0:T(8,128)}, f32[16,16384]{1,0:T(8,128)S(1)}, u32[]{:S(2)}, u32[]{:S(2)}) %collective-permute-start) | collective-permute-done | bytes 1048608 | tf_op jit(solution)/shard_map/ppermute | solution.py:39
  2.9 1.4 broadcast_select_fusion
  4.4 1.8 %collective-permute-start.1 = (f32[2,32,2048]{2,1,0:T(8,128)S(1)}, f32[2,32,2048]{2,1,0:T(8,128)S(1)}, u32[]{:S(2)}, u32[]{:S(2)}) collective-permute-start(f32[2,32,2048]{2,1,0:T(8,128)S(1)} %pad_maximum_fusion.6), channel_id=1, source_target_pairs={{0,2},{1,17},{2,4},{3,19},{4,6},{5,21},{6,0},{7,23},{16,18},{17,33... | collective-permute-start | bytes 1572872 | tf_op jit(solution)/shard_map/ppermute | solution.py:20
  6.2 1.6 collective-permute-start.2
  7.9 2.2 %collective-permute-start.3 = (f32[2,32,2048]{2,1,0:T(8,128)S(1)}, f32[2,32,2048]{2,1,0:T(8,128)}, u32[]{:S(2)}, u32[]{:S(2)}) collective-permute-start(f32[2,32,2048]{2,1,0:T(8,128)S(1)} %pad_maximum_fusion.8), channel_id=1, source_target_pairs={{0,4},{1,33},{2,6},{3,35},{4,0},{5,37},{6,2},{7,39},{16,20},{17,49... | collective-permute-start | bytes 1572872 | tf_op jit(solution)/shard_map/ppermute | solution.py:20
  10.1 4.7 %collective-permute-done.1 = f32[2,32,2048]{2,1,0:T(8,128)S(1)} collective-permute-done((f32[2,32,2048]{2,1,0:T(8,128)S(1)}, f32[2,32,2048]{2,1,0:T(8,128)S(1)}, u32[]{:S(2)}, u32[]{:S(2)}) %collective-permute-start.1) | collective-permute-done | bytes 524320 | tf_op jit(solution)/shard_map/ppermute | solution.py:20
  14.9 0.6 collective-permute-done.2
  15.5 6.5 %collective-permute-done.3 = f32[2,32,2048]{2,1,0:T(8,128)} collective-permute-done((f32[2,32,2048]{2,1,0:T(8,128)S(1)}, f32[2,32,2048]{2,1,0:T(8,128)}, u32[]{:S(2)}, u32[]{:S(2)}) %collective-permute-start.3) | collective-permute-done | bytes 524320 | tf_op jit(solution)/shard_map/ppermute | solution.py:20
  22.0 1.2 pad_maximum_fusion.3
  23.2 0.4 constant_dynamic-slice_fusion
  23.6 2.0 %collective-permute-start.13 = (f32[1,128,2048]{2,1,0:T(8,128)S(1)}, f32[1,128,2048]{2,1,0:T(8,128)S(1)}, u32[]{:S(2)}, u32[]{:S(2)}) collective-permute-start(f32[1,128,2048]{2,1,0:T(8,128)S(1)} %bitcast.32), channel_id=1, source_target_pairs={{0,16},{1,3},{2,18},{3,5},{4,20},{5,7},{6,22},{7,1},{16,32},{17,19... | collective-permute-start | bytes 3145736 | tf_op jit(solution)/shard_map/ppermute | solution.py:29
  25.6 2.2 %collective-permute-start.14 = (f32[1,128,2048]{2,1,0:T(8,128)S(1)}, f32[1,128,2048]{2,1,0:T(8,128)S(1)}, u32[]{:S(2)}, u32[]{:S(2)}) collective-permute-start(f32[1,128,2048]{2,1,0:T(8,128)S(1)} %bitcast.33), channel_id=1, source_target_pairs={{0,48},{1,7},{2,50},{3,1},{4,52},{5,3},{6,54},{7,5},{16,0},{17,23}... | collective-permute-start | bytes 3145736 | tf_op jit(solution)/shard_map/ppermute | solution.py:29
  27.8 12.7 %collective-permute-done.13 = f32[1,128,2048]{2,1,0:T(8,128)S(1)} collective-permute-done((f32[1,128,2048]{2,1,0:T(8,128)S(1)}, f32[1,128,2048]{2,1,0:T(8,128)S(1)}, u32[]{:S(2)}, u32[]{:S(2)}) %collective-permute-start.13) | collective-permute-done | bytes 1048608 | tf_op jit(solution)/shard_map/ppermute | solution.py:29
  40.9 1.9 %collective-permute-start.15 = (f32[1,64,2048]{2,1,0:T(8,128)S(1)}, f32[1,64,2048]{2,1,0:T(8,128)S(1)}, u32[]{:S(2)}, u32[]{:S(2)}) collective-permute-start(f32[1,64,2048]{2,1,0:T(8,128)S(1)} %slice.52), channel_id=1, source_target_pairs={{0,16},{1,3},{2,18},{3,5},{4,20},{5,7},{6,22},{7,1},{16,32},{17,19... | collective-permute-start | bytes 1572872 | tf_op jit(solution)/shard_map/ppermute | solution.py:29
  42.9 2.8 %collective-permute-start.10 = (f32[4,16,2048]{2,1,0:T(8,128)S(1)}, f32[4,16,2048]{2,1,0:T(8,128)S(1)}, u32[]{:S(2)}, u32[]{:S(2)}) collective-permute-start(f32[4,16,2048]{2,1,0:T(8,128)S(1)} %get-tuple-element.45), channel_id=1, source_target_pairs={{0,72},{64,0},{8,64},{72,8},{1,73},{65,1},{9,65},{73,9},{2,74},{66... | collective-permute-start | bytes 1572872 | tf_op jit(solution)/shard_map/ppermute | solution.py:35
  45.7 1.6 collective-permute-start.16
  47.5 4.0 %collective-permute-done.15 = f32[1,64,2048]{2,1,0:T(8,128)S(1)} collective-permute-done((f32[1,64,2048]{2,1,0:T(8,128)S(1)}, f32[1,64,2048]{2,1,0:T(8,128)S(1)}, u32[]{:S(2)}, u32[]{:S(2)}) %collective-permute-start.15) | collective-permute-done | bytes 524320 | tf_op jit(solution)/shard_map/ppermute | solution.py:29
  51.5 3.5 %collective-permute-done.16 = f32[1,64,2048]{2,1,0:T(8,128)S(1)} collective-permute-done((f32[1,64,2048]{2,1,0:T(8,128)S(1)}, f32[1,64,2048]{2,1,0:T(8,128)S(1)}, u32[]{:S(2)}, u32[]{:S(2)}) %collective-permute-start.16) | collective-permute-done | bytes 524320 | tf_op jit(solution)/shard_map/ppermute | solution.py:29
  55.1 1.8 %collective-permute-done.10 = f32[4,16,2048]{2,1,0:T(8,128)S(1)} collective-permute-done((f32[4,16,2048]{2,1,0:T(8,128)S(1)}, f32[4,16,2048]{2,1,0:T(8,128)S(1)}, u32[]{:S(2)}, u32[]{:S(2)}) %collective-permute-start.10) | collective-permute-done | bytes 524320 | tf_op jit(solution)/shard_map/ppermute | solution.py:35
  57.0 5.1 %collective-permute-done.9 = f32[4,16,2048]{2,1,0:T(8,128)S(1)} collective-permute-done((f32[4,16,2048]{2,1,0:T(8,128)S(1)}, f32[4,16,2048]{2,1,0:T(8,128)S(1)}, u32[]{:S(2)}, u32[]{:S(2)}) %collective-permute-start.9) | collective-permute-done | bytes 524320 | tf_op jit(solution)/shard_map/ppermute | solution.py:35
  62.1 1.9 %collective-permute-start.11 = (f32[1,128,2048]{2,1,0:T(8,128)S(1)}, f32[1,128,2048]{2,1,0:T(8,128)S(1)}, u32[]{:S(2)}, u32[]{:S(2)}) collective-permute-start(f32[1,128,2048]{2,1,0:T(8,128)S(1)} %bitcast.38), channel_id=1, source_target_pairs={{0,16},{1,3},{2,18},{3,5},{4,20},{5,7},{6,22},{7,1},{16,32},{17,19... | collective-permute-start | bytes 3145736 | tf_op jit(solution)/shard_map/ppermute | solution.py:29
  64.0 1.6 collective-permute-start.12
  65.6 8.7 %shard_map.17.refs_4_ = f32[2048,1024]{1,0:T(8,128)S(1)} custom-call(s32[1]{0:T(128)} %bitcast.core_ref, f32[3,128,2048]{2,1,0:T(8,128)S(1)} %pad_maximum_fusion.refs_0_, f32[1,128,2048]{2,1,0:T(8,128)S(1)} %constant_dynamic-update-slice_fusion.refs_1_, f32[3,128,2048]{2,1,0:T(8,128)S(1)} %collective-permute-done.17.refs_2_, ...), custom_call_target="tpu_custom_call" | custom-call | flops 6442450944 | bytes 16777216 | tf_op jit(solution)/shard_map/pallas_call | solution.py:106
  74.3 4.0 %collective-permute-done.11 = f32[1,128,2048]{2,1,0:T(8,128)S(1)} collective-permute-done((f32[1,128,2048]{2,1,0:T(8,128)S(1)}, f32[1,128,2048]{2,1,0:T(8,128)S(1)}, u32[]{:S(2)}, u32[]{:S(2)}) %collective-permute-start.11) | collective-permute-done | bytes 1048608 | tf_op jit(solution)/shard_map/ppermute | solution.py:29
  78.3 0.5 collective-permute-done.12
  79.3 3.2 %collective-permute-start.5 = (f32[4,16,2048]{2,1,0:T(8,128)S(1)}, f32[4,16,2048]{2,1,0:T(8,128)S(1)}, u32[]{:S(2)}, u32[]{:S(2)}) collective-permute-start(f32[4,16,2048]{2,1,0:T(8,128)S(1)} %get-tuple-element.46), channel_id=1, source_target_pairs={{0,72},{64,0},{8,64},{72,8},{1,73},{65,1},{9,65},{73,9},{2,74},{66... | collective-permute-start | bytes 1572872 | tf_op jit(solution)/shard_map/ppermute | solution.py:35
  82.6 1.7 collective-permute-start.21
  84.3 10.5 %collective-permute-done.4 = f32[4,16,2048]{2,1,0:T(8,128)S(1)} collective-permute-done((f32[4,16,2048]{2,1,0:T(8,128)S(1)}, f32[4,16,2048]{2,1,0:T(8,128)S(1)}, u32[]{:S(2)}, u32[]{:S(2)}) %collective-permute-start.4) | collective-permute-done | bytes 524320 | tf_op jit(solution)/shard_map/ppermute | solution.py:35
  94.9 1.7 collective-permute-start.7
  96.6 1.6 collective-permute-start.8
  98.2 1.6 collective-permute-start.22
  99.9 1.5 collective-permute-start.6
  101.4 15.6 %collective-permute-done.22 = f32[1,64,2048]{2,1,0:T(8,128)S(1)} collective-permute-done((f32[1,64,2048]{2,1,0:T(8,128)S(1)}, f32[1,64,2048]{2,1,0:T(8,128)S(1)}, u32[]{:S(2)}, u32[]{:S(2)}) %collective-permute-start.22) | collective-permute-done | bytes 524320 | tf_op jit(solution)/shard_map/ppermute | solution.py:29
  117.5 0.6 collective-permute-start.29
  118.2 5.8 %collective-permute-done.6 = f32[4,32,2048]{2,1,0:T(8,128)S(1)} collective-permute-done((f32[4,32,2048]{2,1,0:T(8,128)S(1)}, f32[4,32,2048]{2,1,0:T(8,128)S(1)}, u32[]{:S(2)}, u32[]{:S(2)}) %collective-permute-start.6) | collective-permute-done | bytes 1048608 | tf_op jit(solution)/shard_map/ppermute | solution.py:35
  124.0 1.6 collective-permute-start.19
  125.6 1.6 collective-permute-start.20
  127.3 0.5 collective-permute-start.27
  127.8 2.8 %collective-permute-start.28 = (f32[1,64,2048]{2,1,0:T(8,128)S(1)}, f32[1,64,2048]{2,1,0:T(8,128)S(1)}, u32[]{:S(2)}, u32[]{:S(2)}) collective-permute-start(f32[1,64,2048]{2,1,0:T(8,128)S(1)} %slice.47), channel_id=1, source_target_pairs={{0,48},{1,7},{2,50},{3,1},{4,52},{5,3},{6,54},{7,5},{16,0},{17,23}... | collective-permute-start | bytes 1572872 | tf_op jit(solution)/shard_map/ppermute | solution.py:29
  130.6 8.8 %shard_map.18.refs_4_ = f32[2048,1024]{1,0:T(8,128)S(1)} custom-call(s32[1]{0:T(128)} %bitcast.core_ref, f32[3,128,2048]{2,1,0:T(8,128)S(1)} %pad_maximum_fusion.1.refs_0_, f32[1,128,2048]{2,1,0:T(8,128)S(1)} %constant_dynamic-update-slice_fusion.2.refs_1_, f32[3,128,2048]{2,1,0:T(8,128)S(1)} %collective-permute-done.23.refs_2_, ...), custom_call_target="tpu_custom_call", output_to_operand_aliasing={{}: (5, {})} | custom-call | flops 6442450944 | bytes 16777216 | tf_op jit(solution)/shard_map/pallas_call | solution.py:106
  139.4 6.2 %collective-permute-done.27 = f32[1,64,2048]{2,1,0:T(8,128)S(1)} collective-permute-done((f32[1,64,2048]{2,1,0:T(8,128)S(1)}, f32[1,64,2048]{2,1,0:T(8,128)S(1)}, u32[]{:S(2)}, u32[]{:S(2)}) %collective-permute-start.27) | collective-permute-done | bytes 524320 | tf_op jit(solution)/shard_map/ppermute | solution.py:29
  145.6 0.4 collective-permute-done.28
  146.4 0.6 collective-permute-start.31
  147.1 1.4 collective-permute-start.25
  148.4 1.9 %collective-permute-start.26 = (f32[1,64,2048]{2,1,0:T(8,128)S(1)}, f32[1,64,2048]{2,1,0:T(8,128)S(1)}, u32[]{:S(2)}, u32[]{:S(2)}) collective-permute-start(f32[1,64,2048]{2,1,0:T(8,128)S(1)} %slice.45), channel_id=1, source_target_pairs={{0,48},{1,7},{2,50},{3,1},{4,52},{5,3},{6,54},{7,5},{16,0},{17,23}... | collective-permute-start | bytes 1572872 | tf_op jit(solution)/shard_map/ppermute | solution.py:29
  150.4 8.8 %shard_map.19.refs_4_ = f32[2048,1024]{1,0:T(8,128)S(1)} custom-call(s32[1]{0:T(128)} %bitcast.core_ref, f32[3,128,2048]{2,1,0:T(8,128)S(1)} %pad_maximum_fusion.2.refs_0_, f32[1,128,2048]{2,1,0:T(8,128)S(1)} %constant_dynamic-update-slice_fusion.7.refs_1_, f32[3,128,2048]{2,1,0:T(8,128)S(1)} %collective-permute-done.29.refs_2_, ...), custom_call_target="tpu_custom_call", output_to_operand_aliasing={{}: (5, {})} | custom-call | flops 6442450944 | bytes 16777216 | tf_op jit(solution)/shard_map/pallas_call | solution.py:106
  159.4 2.6 %collective-permute-done.32.refs_3_ = f32[1,128,2048]{2,1,0:T(8,128)S(1)} collective-permute-done((f32[1,128,2048]{2,1,0:T(8,128)S(1)}, f32[1,128,2048]{2,1,0:T(8,128)S(1)}, u32[]{:S(2)}, u32[]{:S(2)}) %collective-permute-start.32) | collective-permute-done | bytes 1048608 | tf_op jit(solution)/shard_map/ppermute | solution.py:39
  162.1 9.8 %shard_map.20 = f32[2048,1024]{1,0:T(8,128)} custom-call(s32[1]{0:T(128)} %bitcast.core_ref, f32[3,128,2048]{2,1,0:T(8,128)S(1)} %constant_dynamic-update-slice_fusion.4.refs_0_, f32[1,128,2048]{2,1,0:T(8,128)S(1)} %constant_dynamic-update-slice_fusion.9.refs_1_, f32[3,128,2048]{2,1,0:T(8,128)S(1)} %collective-permute-done.31.refs_2_, ...), custom_call_target="tpu_custom_call" | custom-call | flops 6442450944 | bytes 16777216 | tf_op jit(solution)/shard_map/pallas_call | solution.py:106
  (57 shorter events, 3.1 us)
Async XLA Ops:
  0.0 2.9 %collective-permute-start = (f32[16,16384]{1,0:T(8,128)}, f32[16,16384]{1,0:T(8,128)S(1)}, u32[]{:S(2)}, u32[]{:S(2)}) collective-permute-start(f32[16,16384]{1,0:T(8,128)} %param.1), channel_id=1, source_target_pairs={{0,1},{1,0},{2,3},{3,2},{4,5},{5,4},{6,7},{7,6},{8,9},{9,8},{10,11... | collective-permute-start | bytes 3145736 | tf_op jit(solution)/shard_map/ppermute | solution.py:39
  4.4 10.5 %collective-permute-start.1 = (f32[2,32,2048]{2,1,0:T(8,128)S(1)}, f32[2,32,2048]{2,1,0:T(8,128)S(1)}, u32[]{:S(2)}, u32[]{:S(2)}) collective-permute-start(f32[2,32,2048]{2,1,0:T(8,128)S(1)} %pad_maximum_fusion.6), channel_id=1, source_target_pairs={{0,2},{1,17},{2,4},{3,19},{4,6},{5,21},{6,0},{7,23},{16,18},{17,33... | collective-permute-start | bytes 1572872 | tf_op jit(solution)/shard_map/ppermute | solution.py:20
  6.2 9.2 %collective-permute-start.2 = (f32[2,32,2048]{2,1,0:T(8,128)S(1)}, f32[2,32,2048]{2,1,0:T(8,128)S(1)}, u32[]{:S(2)}, u32[]{:S(2)}) collective-permute-start(f32[2,32,2048]{2,1,0:T(8,128)S(1)} %pad_maximum_fusion.7), channel_id=1, source_target_pairs={{0,6},{1,49},{2,0},{3,51},{4,2},{5,53},{6,4},{7,55},{16,22},{17,1}... | collective-permute-start | bytes 1572872 | tf_op jit(solution)/shard_map/ppermute | solution.py:20
  7.9 14.0 %collective-permute-start.3 = (f32[2,32,2048]{2,1,0:T(8,128)S(1)}, f32[2,32,2048]{2,1,0:T(8,128)}, u32[]{:S(2)}, u32[]{:S(2)}) collective-permute-start(f32[2,32,2048]{2,1,0:T(8,128)S(1)} %pad_maximum_fusion.8), channel_id=1, source_target_pairs={{0,4},{1,33},{2,6},{3,35},{4,0},{5,37},{6,2},{7,39},{16,20},{17,49... | collective-permute-start | bytes 1572872 | tf_op jit(solution)/shard_map/ppermute | solution.py:20
  23.6 16.9 %collective-permute-start.13 = (f32[1,128,2048]{2,1,0:T(8,128)S(1)}, f32[1,128,2048]{2,1,0:T(8,128)S(1)}, u32[]{:S(2)}, u32[]{:S(2)}) collective-permute-start(f32[1,128,2048]{2,1,0:T(8,128)S(1)} %bitcast.32), channel_id=1, source_target_pairs={{0,16},{1,3},{2,18},{3,5},{4,20},{5,7},{6,22},{7,1},{16,32},{17,19... | collective-permute-start | bytes 3145736 | tf_op jit(solution)/shard_map/ppermute | solution.py:29
  25.6 14.9 %collective-permute-start.14 = (f32[1,128,2048]{2,1,0:T(8,128)S(1)}, f32[1,128,2048]{2,1,0:T(8,128)S(1)}, u32[]{:S(2)}, u32[]{:S(2)}) collective-permute-start(f32[1,128,2048]{2,1,0:T(8,128)S(1)} %bitcast.33), channel_id=1, source_target_pairs={{0,48},{1,7},{2,50},{3,1},{4,52},{5,3},{6,54},{7,5},{16,0},{17,23}... | collective-permute-start | bytes 3145736 | tf_op jit(solution)/shard_map/ppermute | solution.py:29
  40.8 24.8 %collective-permute-start.17 = (f32[3,128,2048]{2,1,0:T(8,128)S(1)}, f32[3,128,2048]{2,1,0:T(8,128)S(1)}, u32[]{:S(2)}, u32[]{:S(2)}) collective-permute-start(f32[3,128,2048]{2,1,0:T(8,128)S(1)} %pad_maximum_fusion.refs_0_), channel_id=1, source_target_pairs={{0,1},{1,0},{2,3},{3,2},{4,5},{5,4},{6,7},{7,6},{8,9},{9,8},{10,11... | collective-permute-start | bytes 9437192 | tf_op jit(solution)/shard_map/ppermute | solution.py:39
  40.9 10.5 %collective-permute-start.15 = (f32[1,64,2048]{2,1,0:T(8,128)S(1)}, f32[1,64,2048]{2,1,0:T(8,128)S(1)}, u32[]{:S(2)}, u32[]{:S(2)}) collective-permute-start(f32[1,64,2048]{2,1,0:T(8,128)S(1)} %slice.52), channel_id=1, source_target_pairs={{0,16},{1,3},{2,18},{3,5},{4,20},{5,7},{6,22},{7,1},{16,32},{17,19... | collective-permute-start | bytes 1572872 | tf_op jit(solution)/shard_map/ppermute | solution.py:29
  42.9 14.1 %collective-permute-start.10 = (f32[4,16,2048]{2,1,0:T(8,128)S(1)}, f32[4,16,2048]{2,1,0:T(8,128)S(1)}, u32[]{:S(2)}, u32[]{:S(2)}) collective-permute-start(f32[4,16,2048]{2,1,0:T(8,128)S(1)} %get-tuple-element.45), channel_id=1, source_target_pairs={{0,72},{64,0},{8,64},{72,8},{1,73},{65,1},{9,65},{73,9},{2,74},{66... | collective-permute-start | bytes 1572872 | tf_op jit(solution)/shard_map/ppermute | solution.py:35
  45.7 9.3 %collective-permute-start.16 = (f32[1,64,2048]{2,1,0:T(8,128)S(1)}, f32[1,64,2048]{2,1,0:T(8,128)S(1)}, u32[]{:S(2)}, u32[]{:S(2)}) collective-permute-start(f32[1,64,2048]{2,1,0:T(8,128)S(1)} %slice.53), channel_id=1, source_target_pairs={{0,48},{1,7},{2,50},{3,1},{4,52},{5,3},{6,54},{7,5},{16,0},{17,23}... | collective-permute-start | bytes 1572872 | tf_op jit(solution)/shard_map/ppermute | solution.py:29
  47.4 14.7 %collective-permute-start.9 = (f32[4,16,2048]{2,1,0:T(8,128)S(1)}, f32[4,16,2048]{2,1,0:T(8,128)S(1)}, u32[]{:S(2)}, u32[]{:S(2)}) collective-permute-start(f32[4,16,2048]{2,1,0:T(8,128)S(1)} %get-tuple-element.43), channel_id=1, source_target_pairs={{0,64},{64,8},{8,72},{72,0},{1,65},{65,9},{9,73},{73,1},{2,66},{66... | collective-permute-start | bytes 1572872 | tf_op jit(solution)/shard_map/ppermute | solution.py:35
  55.0 10.6 %collective-permute-start.18 = (f32[1,128,2048]{2,1,0:T(8,128)S(1)}, f32[1,128,2048]{2,1,0:T(8,128)S(1)}, u32[]{:S(2)}, u32[]{:S(2)}) collective-permute-start(f32[1,128,2048]{2,1,0:T(8,128)S(1)} %constant_dynamic-update-slice_fusion.refs_1_), channel_id=1, source_target_pairs={{0,1},{1,0},{2,3},{3,2},{4,5},{5,4},{6,7},{7,6},{8,9},{9,8},{10,11... | collective-permute-start | bytes 3145736 | tf_op jit(solution)/shard_map/ppermute | solution.py:39
  62.1 16.2 %collective-permute-start.11 = (f32[1,128,2048]{2,1,0:T(8,128)S(1)}, f32[1,128,2048]{2,1,0:T(8,128)S(1)}, u32[]{:S(2)}, u32[]{:S(2)}) collective-permute-start(f32[1,128,2048]{2,1,0:T(8,128)S(1)} %bitcast.38), channel_id=1, source_target_pairs={{0,16},{1,3},{2,18},{3,5},{4,20},{5,7},{6,22},{7,1},{16,32},{17,19... | collective-permute-start | bytes 3145736 | tf_op jit(solution)/shard_map/ppermute | solution.py:29
  64.0 14.8 %collective-permute-start.12 = (f32[1,128,2048]{2,1,0:T(8,128)S(1)}, f32[1,128,2048]{2,1,0:T(8,128)S(1)}, u32[]{:S(2)}, u32[]{:S(2)}) collective-permute-start(f32[1,128,2048]{2,1,0:T(8,128)S(1)} %bitcast.39), channel_id=1, source_target_pairs={{0,48},{1,7},{2,50},{3,1},{4,52},{5,3},{6,54},{7,5},{16,0},{17,23}... | collective-permute-start | bytes 3145736 | tf_op jit(solution)/shard_map/ppermute | solution.py:29
  79.2 48.6 %collective-permute-start.23 = (f32[3,128,2048]{2,1,0:T(8,128)S(1)}, f32[3,128,2048]{2,1,0:T(8,128)S(1)}, u32[]{:S(2)}, u32[]{:S(2)}) collective-permute-start(f32[3,128,2048]{2,1,0:T(8,128)S(1)} %pad_maximum_fusion.1.refs_0_), channel_id=1, source_target_pairs={{0,1},{1,0},{2,3},{3,2},{4,5},{5,4},{6,7},{7,6},{8,9},{9,8},{10,11... | collective-permute-start | bytes 9437192 | tf_op jit(solution)/shard_map/ppermute | solution.py:39
  79.3 15.5 %collective-permute-start.4 = (f32[4,16,2048]{2,1,0:T(8,128)S(1)}, f32[4,16,2048]{2,1,0:T(8,128)S(1)}, u32[]{:S(2)}, u32[]{:S(2)}) collective-permute-start(f32[4,16,2048]{2,1,0:T(8,128)S(1)} %get-tuple-element.44), channel_id=1, source_target_pairs={{0,64},{64,8},{8,72},{72,0},{1,65},{65,9},{9,73},{73,1},{2,66},{66... | collective-permute-start | bytes 1572872 | tf_op jit(solution)/shard_map/ppermute | solution.py:35
  79.3 15.5 %collective-permute-start.5 = (f32[4,16,2048]{2,1,0:T(8,128)S(1)}, f32[4,16,2048]{2,1,0:T(8,128)S(1)}, u32[]{:S(2)}, u32[]{:S(2)}) collective-permute-start(f32[4,16,2048]{2,1,0:T(8,128)S(1)} %get-tuple-element.46), channel_id=1, source_target_pairs={{0,72},{64,0},{8,64},{72,8},{1,73},{65,1},{9,65},{73,9},{2,74},{66... | collective-permute-start | bytes 1572872 | tf_op jit(solution)/shard_map/ppermute | solution.py:35
  82.6 17.3 %collective-permute-start.21 = (f32[1,64,2048]{2,1,0:T(8,128)S(1)}, f32[1,64,2048]{2,1,0:T(8,128)S(1)}, u32[]{:S(2)}, u32[]{:S(2)}) collective-permute-start(f32[1,64,2048]{2,1,0:T(8,128)S(1)} %slice.42), channel_id=1, source_target_pairs={{0,16},{1,3},{2,18},{3,5},{4,20},{5,7},{6,22},{7,1},{16,32},{17,19... | collective-permute-start | bytes 1572872 | tf_op jit(solution)/shard_map/ppermute | solution.py:29
  94.9 22.2 %collective-permute-start.7 = (f32[1,128,2048]{2,1,0:T(8,128)S(1)}, f32[1,128,2048]{2,1,0:T(8,128)S(1)}, u32[]{:S(2)}, u32[]{:S(2)}) collective-permute-start(f32[1,128,2048]{2,1,0:T(8,128)S(1)} %bitcast.35), channel_id=1, source_target_pairs={{0,16},{1,3},{2,18},{3,5},{4,20},{5,7},{6,22},{7,1},{16,32},{17,19... | collective-permute-start | bytes 3145736 | tf_op jit(solution)/shard_map/ppermute | solution.py:29
  96.6 20.6 %collective-permute-start.8 = (f32[1,128,2048]{2,1,0:T(8,128)S(1)}, f32[1,128,2048]{2,1,0:T(8,128)S(1)}, u32[]{:S(2)}, u32[]{:S(2)}) collective-permute-start(f32[1,128,2048]{2,1,0:T(8,128)S(1)} %bitcast.36), channel_id=1, source_target_pairs={{0,48},{1,7},{2,50},{3,1},{4,52},{5,3},{6,54},{7,5},{16,0},{17,23}... | collective-permute-start | bytes 3145736 | tf_op jit(solution)/shard_map/ppermute | solution.py:29
  98.2 18.8 %collective-permute-start.22 = (f32[1,64,2048]{2,1,0:T(8,128)S(1)}, f32[1,64,2048]{2,1,0:T(8,128)S(1)}, u32[]{:S(2)}, u32[]{:S(2)}) collective-permute-start(f32[1,64,2048]{2,1,0:T(8,128)S(1)} %slice.43), channel_id=1, source_target_pairs={{0,48},{1,7},{2,50},{3,1},{4,52},{5,3},{6,54},{7,5},{16,0},{17,23}... | collective-permute-start | bytes 1572872 | tf_op jit(solution)/shard_map/ppermute | solution.py:29
  99.9 24.1 %collective-permute-start.6 = (f32[4,32,2048]{2,1,0:T(8,128)S(1)}, f32[4,32,2048]{2,1,0:T(8,128)S(1)}, u32[]{:S(2)}, u32[]{:S(2)}) collective-permute-start(f32[4,32,2048]{2,1,0:T(8,128)S(1)} %get-tuple-element.17), channel_id=1, source_target_pairs={{0,8},{64,72},{8,0},{72,64},{1,9},{65,73},{9,1},{73,65},{2,10},{66... | collective-permute-start | bytes 3145736 | tf_op jit(solution)/shard_map/ppermute | solution.py:35
  117.1 10.3 %collective-permute-start.24 = (f32[1,128,2048]{2,1,0:T(8,128)S(1)}, f32[1,128,2048]{2,1,0:T(8,128)S(1)}, u32[]{:S(2)}, u32[]{:S(2)}) collective-permute-start(f32[1,128,2048]{2,1,0:T(8,128)S(1)} %constant_dynamic-update-slice_fusion.2.refs_1_), channel_id=1, source_target_pairs={{0,1},{1,0},{2,3},{3,2},{4,5},{5,4},{6,7},{7,6},{8,9},{9,8},{10,11... | collective-permute-start | bytes 3145736 | tf_op jit(solution)/shard_map/ppermute | solution.py:39
  117.5 32.9 %collective-permute-start.29 = (f32[3,128,2048]{2,1,0:T(8,128)S(1)}, f32[3,128,2048]{2,1,0:T(8,128)S(1)}, u32[]{:S(2)}, u32[]{:S(2)}) collective-permute-start(f32[3,128,2048]{2,1,0:T(8,128)S(1)} %pad_maximum_fusion.2.refs_0_), channel_id=1, source_target_pairs={{0,1},{1,0},{2,3},{3,2},{4,5},{5,4},{6,7},{7,6},{8,9},{9,8},{10,11... | collective-permute-start | bytes 9437192 | tf_op jit(solution)/shard_map/ppermute | solution.py:39
  124.0 22.2 %collective-permute-start.19 = (f32[1,128,2048]{2,1,0:T(8,128)S(1)}, f32[1,128,2048]{2,1,0:T(8,128)S(1)}, u32[]{:S(2)}, u32[]{:S(2)}) collective-permute-start(f32[1,128,2048]{2,1,0:T(8,128)S(1)} %bitcast.41), channel_id=1, source_target_pairs={{0,16},{1,3},{2,18},{3,5},{4,20},{5,7},{6,22},{7,1},{16,32},{17,19... | collective-permute-start | bytes 3145736 | tf_op jit(solution)/shard_map/ppermute | solution.py:29
  125.6 20.6 %collective-permute-start.20 = (f32[1,128,2048]{2,1,0:T(8,128)S(1)}, f32[1,128,2048]{2,1,0:T(8,128)S(1)}, u32[]{:S(2)}, u32[]{:S(2)}) collective-permute-start(f32[1,128,2048]{2,1,0:T(8,128)S(1)} %bitcast.42), channel_id=1, source_target_pairs={{0,48},{1,7},{2,50},{3,1},{4,52},{5,3},{6,54},{7,5},{16,0},{17,23}... | collective-permute-start | bytes 3145736 | tf_op jit(solution)/shard_map/ppermute | solution.py:29
  127.3 18.3 %collective-permute-start.27 = (f32[1,64,2048]{2,1,0:T(8,128)S(1)}, f32[1,64,2048]{2,1,0:T(8,128)S(1)}, u32[]{:S(2)}, u32[]{:S(2)}) collective-permute-start(f32[1,64,2048]{2,1,0:T(8,128)S(1)} %slice.46), channel_id=1, source_target_pairs={{0,16},{1,3},{2,18},{3,5},{4,20},{5,7},{6,22},{7,1},{16,32},{17,19... | collective-permute-start | bytes 1572872 | tf_op jit(solution)/shard_map/ppermute | solution.py:29
  127.8 18.2 %collective-permute-start.28 = (f32[1,64,2048]{2,1,0:T(8,128)S(1)}, f32[1,64,2048]{2,1,0:T(8,128)S(1)}, u32[]{:S(2)}, u32[]{:S(2)}) collective-permute-start(f32[1,64,2048]{2,1,0:T(8,128)S(1)} %slice.47), channel_id=1, source_target_pairs={{0,48},{1,7},{2,50},{3,1},{4,52},{5,3},{6,54},{7,5},{16,0},{17,23}... | collective-permute-start | bytes 1572872 | tf_op jit(solution)/shard_map/ppermute | solution.py:29
  146.1 4.3 %collective-permute-start.30 = (f32[1,128,2048]{2,1,0:T(8,128)S(1)}, f32[1,128,2048]{2,1,0:T(8,128)S(1)}, u32[]{:S(2)}, u32[]{:S(2)}) collective-permute-start(f32[1,128,2048]{2,1,0:T(8,128)S(1)} %constant_dynamic-update-slice_fusion.7.refs_1_), channel_id=1, source_target_pairs={{0,1},{1,0},{2,3},{3,2},{4,5},{5,4},{6,7},{7,6},{8,9},{9,8},{10,11... | collective-permute-start | bytes 3145736 | tf_op jit(solution)/shard_map/ppermute | solution.py:39
  146.4 15.7 %collective-permute-start.31 = (f32[3,128,2048]{2,1,0:T(8,128)S(1)}, f32[3,128,2048]{2,1,0:T(8,128)S(1)}, u32[]{:S(2)}, u32[]{:S(2)}) collective-permute-start(f32[3,128,2048]{2,1,0:T(8,128)S(1)} %constant_dynamic-update-slice_fusion.4.refs_0_), channel_id=1, source_target_pairs={{0,1},{1,0},{2,3},{3,2},{4,5},{5,4},{6,7},{7,6},{8,9},{9,8},{10,11... | collective-permute-start | bytes 9437192 | tf_op jit(solution)/shard_map/ppermute | solution.py:39
  147.1 12.2 %collective-permute-start.25 = (f32[1,64,2048]{2,1,0:T(8,128)S(1)}, f32[1,64,2048]{2,1,0:T(8,128)S(1)}, u32[]{:S(2)}, u32[]{:S(2)}) collective-permute-start(f32[1,64,2048]{2,1,0:T(8,128)S(1)} %slice.44), channel_id=1, source_target_pairs={{0,16},{1,3},{2,18},{3,5},{4,20},{5,7},{6,22},{7,1},{16,32},{17,19... | collective-permute-start | bytes 1572872 | tf_op jit(solution)/shard_map/ppermute | solution.py:29
  148.4 10.8 %collective-permute-start.26 = (f32[1,64,2048]{2,1,0:T(8,128)S(1)}, f32[1,64,2048]{2,1,0:T(8,128)S(1)}, u32[]{:S(2)}, u32[]{:S(2)}) collective-permute-start(f32[1,64,2048]{2,1,0:T(8,128)S(1)} %slice.45), channel_id=1, source_target_pairs={{0,48},{1,7},{2,50},{3,1},{4,52},{5,3},{6,54},{7,5},{16,0},{17,23}... | collective-permute-start | bytes 1572872 | tf_op jit(solution)/shard_map/ppermute | solution.py:29
  159.3 2.7 %collective-permute-start.32 = (f32[1,128,2048]{2,1,0:T(8,128)S(1)}, f32[1,128,2048]{2,1,0:T(8,128)S(1)}, u32[]{:S(2)}, u32[]{:S(2)}) collective-permute-start(f32[1,128,2048]{2,1,0:T(8,128)S(1)} %constant_dynamic-update-slice_fusion.9.refs_1_), channel_id=1, source_target_pairs={{0,1},{1,0},{2,3},{3,2},{4,5},{5,4},{6,7},{7,6},{8,9},{9,8},{10,11... | collective-permute-start | bytes 3145736 | tf_op jit(solution)/shard_map/ppermute | solution.py:39

commit v3 on v2

--- a/solution.py
+++ b/solution.py
@@ -172,24 +172,26 @@
         mine = (jnp.concatenate(near), jnp.concatenate(ends, axis=1))
         return mine, (swap(mine[0]), swap(mine[1]))
 
+    def add(slices, total, scale=None):
+        return gram_add(core, *slices, total, scale)
+
     own_1 = begin(own)
     own_2 = forward(*own_1)
     left_1 = begin(left)
     right_1 = begin(right)
-    total = gram_add(core, *finish([own, *own_1], own_2), None)
-    left_1 = after(left_1, [total])
     left_2 = forward(*left_1)
-    right_1 = after(right_1, left_1)
+    total = add(finish([own, *own_1], own_2), None)
+    right_1 = after(right_1, [total])
     right_2 = forward(*right_1)
-    (far,) = after([far], right_1)
+    (far,) = after([far], [total])
     far_1 = begin(far)
-    total = gram_add(core, *finish([left, *left_1], left_2), total)
-    right_2 = after(right_2, [total])
+    total = add(finish([left, *left_1], left_2), total)
+    right_2 = after(right_2, left_2)
     far_1 = after(far_1, [total])
     far_2 = forward(*far_1)
-    total = gram_add(core, *finish([right, *right_1], right_2), total)
+    total = add(finish([right, *right_1], right_2), total)
     far_2 = after(far_2, [total])
-    return gram_add(core, *finish([far, *far_1], far_2), total, 1 / (rows * 128))
+    return add(finish([far, *far_1], far_2), total, 1 / (rows * 128))
 
 
 def solution(mesh):

time: 173 us -> 162 us (0.936)
  waiting for transfers between devices: 87.5 us -> 72.1 us
  starting transfers between devices: 42.4 us -> 46.3 us
    ppermute x16, waiting for transfers between devices: 46.9 us -> 35.6 us  [move_ring(): return lax.ppermute(value, ('z', 'y', 'core'), pairs)]
    ppermute x5, waiting for transfers between devices: 23.3 us -> 19.1 us  [move_x(): return lax.ppermute(value, ('xl', 'xh'), pairs)]
    ppermute x5, starting transfers between devices: 7.66 us -> 10.7 us  [move_x(): return lax.ppermute(value, ('xl', 'xh'), pairs)]
  transfers between devices with their start and end apart: 33 -> 33, of which waited for: 17 -> 18; matrix products, arithmetic and copies ran while one was open for 1% -> 1% of each run, Pallas kernels for 15% -> 16%
where the time goes in v3:
time: 162 us; the launch traced here: 160 us
  waiting for transfers between devices  72.1 us (45%)
  starting transfers between devices  46.3 us (29%)
  Pallas kernels  36.2 us (22%)
  other arithmetic  4.08 us (3%)
    pallas_call x4, Pallas kernels, gram_add(): pl.pallas_call(functools.partial(gram_kernel, scale=scale, tile=tile, las...  36.2 us
    ppermute x16, waiting for transfers between devices, move_ring(): return lax.ppermute(value, ('z', 'y', 'core'), pairs)  35.6 us
    ppermute x16, starting transfers between devices, move_ring(): return lax.ppermute(value, ('z', 'y', 'core'), pairs)  29 us
    ppermute x5, waiting for transfers between devices, move_x(): return lax.ppermute(value, ('xl', 'xh'), pairs)  19.1 us
    ppermute x3, waiting for transfers between devices, move(): return lax.ppermute(value, ('z', 'y', 'core'), pairs)  11.8 us
    ppermute x5, starting transfers between devices, move_x(): return lax.ppermute(value, ('xl', 'xh'), pairs)  10.7 us
    ppermute x3, starting transfers between devices, move(): return lax.ppermute(value, ('z', 'y', 'core'), pairs)  5.55 us
    ppermute x9, waiting for transfers between devices, swap(): return lax.ppermute(value, 'core', [(0, 1), (1, 0)])  5.53 us
  transfers between devices with their start and end apart: 33, of which 18 were waited for; matrix products, arithmetic and copies ran while one was open for 1% of the time, Pallas kernels for 16%

profile of v3, /device:TPU:0, one launch (start us, length us, event | category | flops | bytes accessed | tf_op | source)
XLA Modules:
  0.0 160.4 jit_solution(17664644157301675458)
XLA Ops:
  0.0 2.9 %collective-permute-done = f32[16,16384]{1,0:T(8,128)S(1)} collective-permute-done((f32[16,16384]{1,0:T(8,128)}, f32[16,16384]{1,0:T(8,128)S(1)}, u32[]{:S(2)}, u32[]{:S(2)}) %collective-permute-start) | collective-permute-done | bytes 1048608 | tf_op jit(solution)/shard_map/ppermute | solution.py:39
  2.9 1.4 broadcast_select_fusion
  4.4 1.8 %collective-permute-start.1 = (f32[2,32,2048]{2,1,0:T(8,128)S(1)}, f32[2,32,2048]{2,1,0:T(8,128)S(1)}, u32[]{:S(2)}, u32[]{:S(2)}) collective-permute-start(f32[2,32,2048]{2,1,0:T(8,128)S(1)} %pad_maximum_fusion.6), channel_id=1, source_target_pairs={{0,2},{1,17},{2,4},{3,19},{4,6},{5,21},{6,0},{7,23},{16,18},{17,33... | collective-permute-start | bytes 1572872 | tf_op jit(solution)/shard_map/ppermute | solution.py:20
  6.2 1.6 %collective-permute-start.2 = (f32[2,32,2048]{2,1,0:T(8,128)S(1)}, f32[2,32,2048]{2,1,0:T(8,128)S(1)}, u32[]{:S(2)}, u32[]{:S(2)}) collective-permute-start(f32[2,32,2048]{2,1,0:T(8,128)S(1)} %pad_maximum_fusion.7), channel_id=1, source_target_pairs={{0,6},{1,49},{2,0},{3,51},{4,2},{5,53},{6,4},{7,55},{16,22},{17,1}... | collective-permute-start | bytes 1572872 | tf_op jit(solution)/shard_map/ppermute | solution.py:20
  7.9 2.2 %collective-permute-start.3 = (f32[2,32,2048]{2,1,0:T(8,128)S(1)}, f32[2,32,2048]{2,1,0:T(8,128)}, u32[]{:S(2)}, u32[]{:S(2)}) collective-permute-start(f32[2,32,2048]{2,1,0:T(8,128)S(1)} %pad_maximum_fusion.8), channel_id=1, source_target_pairs={{0,4},{1,33},{2,6},{3,35},{4,0},{5,37},{6,2},{7,39},{16,20},{17,49... | collective-permute-start | bytes 1572872 | tf_op jit(solution)/shard_map/ppermute | solution.py:20
  10.1 4.7 %collective-permute-done.1 = f32[2,32,2048]{2,1,0:T(8,128)S(1)} collective-permute-done((f32[2,32,2048]{2,1,0:T(8,128)S(1)}, f32[2,32,2048]{2,1,0:T(8,128)S(1)}, u32[]{:S(2)}, u32[]{:S(2)}) %collective-permute-start.1) | collective-permute-done | bytes 524320 | tf_op jit(solution)/shard_map/ppermute | solution.py:20
  14.9 0.6 collective-permute-done.2
  15.5 6.5 %collective-permute-done.3 = f32[2,32,2048]{2,1,0:T(8,128)} collective-permute-done((f32[2,32,2048]{2,1,0:T(8,128)S(1)}, f32[2,32,2048]{2,1,0:T(8,128)}, u32[]{:S(2)}, u32[]{:S(2)}) %collective-permute-start.3) | collective-permute-done | bytes 524320 | tf_op jit(solution)/shard_map/ppermute | solution.py:20
  22.0 1.2 pad_maximum_fusion.3
  23.2 0.4 constant_dynamic-slice_fusion
  23.7 2.0 %collective-permute-start.7 = (f32[1,128,2048]{2,1,0:T(8,128)S(1)}, f32[1,128,2048]{2,1,0:T(8,128)S(1)}, u32[]{:S(2)}, u32[]{:S(2)}) collective-permute-start(f32[1,128,2048]{2,1,0:T(8,128)S(1)} %bitcast.32), channel_id=1, source_target_pairs={{0,16},{1,3},{2,18},{3,5},{4,20},{5,7},{6,22},{7,1},{16,32},{17,19... | collective-permute-start | bytes 3145736 | tf_op jit(solution)/shard_map/ppermute | solution.py:29
  25.7 2.2 %collective-permute-start.8 = (f32[1,128,2048]{2,1,0:T(8,128)S(1)}, f32[1,128,2048]{2,1,0:T(8,128)S(1)}, u32[]{:S(2)}, u32[]{:S(2)}) collective-permute-start(f32[1,128,2048]{2,1,0:T(8,128)S(1)} %bitcast.33), channel_id=1, source_target_pairs={{0,48},{1,7},{2,50},{3,1},{4,52},{5,3},{6,54},{7,5},{16,0},{17,23}... | collective-permute-start | bytes 3145736 | tf_op jit(solution)/shard_map/ppermute | solution.py:29
  27.9 1.6 collective-permute-start.15
  29.6 1.8 %collective-permute-start.16 = (f32[4,16,2048]{2,1,0:T(8,128)S(1)}, f32[4,16,2048]{2,1,0:T(8,128)S(1)}, u32[]{:S(2)}, u32[]{:S(2)}) collective-permute-start(f32[4,16,2048]{2,1,0:T(8,128)S(1)} %get-tuple-element.41), channel_id=1, source_target_pairs={{0,72},{64,0},{8,64},{72,8},{1,73},{65,1},{9,65},{73,9},{2,74},{66... | collective-permute-start | bytes 1572872 | tf_op jit(solution)/shard_map/ppermute | solution.py:35
  31.4 9.2 %collective-permute-done.7 = f32[1,128,2048]{2,1,0:T(8,128)S(1)} collective-permute-done((f32[1,128,2048]{2,1,0:T(8,128)S(1)}, f32[1,128,2048]{2,1,0:T(8,128)S(1)}, u32[]{:S(2)}, u32[]{:S(2)}) %collective-permute-start.7) | collective-permute-done | bytes 1048608 | tf_op jit(solution)/shard_map/ppermute | solution.py:29
  40.6 0.3 pad_maximum_fusion.refs_0_
  41.0 0.8 collective-permute-done.15
  42.0 1.5 collective-permute-start.17
  43.5 1.8 %collective-permute-start.18 = (f32[1,128,2048]{2,1,0:T(8,128)S(1)}, f32[1,128,2048]{2,1,0:T(8,128)S(1)}, u32[]{:S(2)}, u32[]{:S(2)}) collective-permute-start(f32[1,128,2048]{2,1,0:T(8,128)S(1)} %bitcast.39), channel_id=1, source_target_pairs={{0,48},{1,7},{2,50},{3,1},{4,52},{5,3},{6,54},{7,5},{16,0},{17,23}... | collective-permute-start | bytes 3145736 | tf_op jit(solution)/shard_map/ppermute | solution.py:29
  45.6 3.1 %collective-permute-start.10 = (f32[1,64,2048]{2,1,0:T(8,128)S(1)}, f32[1,64,2048]{2,1,0:T(8,128)S(1)}, u32[]{:S(2)}, u32[]{:S(2)}) collective-permute-start(f32[1,64,2048]{2,1,0:T(8,128)S(1)} %slice.51), channel_id=1, source_target_pairs={{0,48},{1,7},{2,50},{3,1},{4,52},{5,3},{6,54},{7,5},{16,0},{17,23}... | collective-permute-start | bytes 1572872 | tf_op jit(solution)/shard_map/ppermute | solution.py:29
  48.7 9.3 %collective-permute-done.17 = f32[1,128,2048]{2,1,0:T(8,128)S(1)} collective-permute-done((f32[1,128,2048]{2,1,0:T(8,128)S(1)}, f32[1,128,2048]{2,1,0:T(8,128)S(1)}, u32[]{:S(2)}, u32[]{:S(2)}) %collective-permute-start.17) | collective-permute-done | bytes 1048608 | tf_op jit(solution)/shard_map/ppermute | solution.py:29
  58.3 0.3 pad_maximum_fusion.1.refs_0_
  58.7 1.6 collective-permute-start.4
  60.3 3.4 %collective-permute-done.9 = f32[1,64,2048]{2,1,0:T(8,128)S(1)} collective-permute-done((f32[1,64,2048]{2,1,0:T(8,128)S(1)}, f32[1,64,2048]{2,1,0:T(8,128)S(1)}, u32[]{:S(2)}, u32[]{:S(2)}) %collective-permute-start.9) | collective-permute-done | bytes 524320 | tf_op jit(solution)/shard_map/ppermute | solution.py:29
  63.7 3.0 %collective-permute-start.5 = (f32[4,16,2048]{2,1,0:T(8,128)S(1)}, f32[4,16,2048]{2,1,0:T(8,128)S(1)}, u32[]{:S(2)}, u32[]{:S(2)}) collective-permute-start(f32[4,16,2048]{2,1,0:T(8,128)S(1)} %get-tuple-element.42), channel_id=1, source_target_pairs={{0,72},{64,0},{8,64},{72,8},{1,73},{65,1},{9,65},{73,9},{2,74},{66... | collective-permute-start | bytes 1572872 | tf_op jit(solution)/shard_map/ppermute | solution.py:35
  66.9 7.3 %collective-permute-done.4 = f32[4,16,2048]{2,1,0:T(8,128)S(1)} collective-permute-done((f32[4,16,2048]{2,1,0:T(8,128)S(1)}, f32[4,16,2048]{2,1,0:T(8,128)S(1)}, u32[]{:S(2)}, u32[]{:S(2)}) %collective-permute-start.4) | collective-permute-done | bytes 524320 | tf_op jit(solution)/shard_map/ppermute | solution.py:35
  74.2 1.1 collective-permute-start.19
  75.4 1.1 collective-permute-done.5
  76.5 3.3 %collective-permute-start.20 = (f32[1,64,2048]{2,1,0:T(8,128)S(1)}, f32[1,64,2048]{2,1,0:T(8,128)S(1)}, u32[]{:S(2)}, u32[]{:S(2)}) collective-permute-start(f32[1,64,2048]{2,1,0:T(8,128)S(1)} %slice.55), channel_id=1, source_target_pairs={{0,48},{1,7},{2,50},{3,1},{4,52},{5,3},{6,54},{7,5},{16,0},{17,23}... | collective-permute-start | bytes 1572872 | tf_op jit(solution)/shard_map/ppermute | solution.py:29
  79.9 4.7 %collective-permute-done.19 = f32[1,64,2048]{2,1,0:T(8,128)S(1)} collective-permute-done((f32[1,64,2048]{2,1,0:T(8,128)S(1)}, f32[1,64,2048]{2,1,0:T(8,128)S(1)}, u32[]{:S(2)}, u32[]{:S(2)}) %collective-permute-start.19) | collective-permute-done | bytes 524320 | tf_op jit(solution)/shard_map/ppermute | solution.py:29
  84.6 1.9 %collective-permute-done.20 = f32[1,64,2048]{2,1,0:T(8,128)S(1)} collective-permute-done((f32[1,64,2048]{2,1,0:T(8,128)S(1)}, f32[1,64,2048]{2,1,0:T(8,128)S(1)}, u32[]{:S(2)}, u32[]{:S(2)}) %collective-permute-start.20) | collective-permute-done | bytes 524320 | tf_op jit(solution)/shard_map/ppermute | solution.py:29
  86.5 3.7 %collective-permute-start.26 = (f32[1,128,2048]{2,1,0:T(8,128)S(1)}, f32[1,128,2048]{2,1,0:T(8,128)S(1)}, u32[]{:S(2)}, u32[]{:S(2)}) collective-permute-start(f32[1,128,2048]{2,1,0:T(8,128)S(1)} %bitcast.36), channel_id=1, source_target_pairs={{0,48},{1,7},{2,50},{3,1},{4,52},{5,3},{6,54},{7,5},{16,0},{17,23}... | collective-permute-start | bytes 3145736 | tf_op jit(solution)/shard_map/ppermute | solution.py:29
  90.3 2.8 %collective-permute-start.6 = (f32[4,32,2048]{2,1,0:T(8,128)S(1)}, f32[4,32,2048]{2,1,0:T(8,128)S(1)}, u32[]{:S(2)}, u32[]{:S(2)}) collective-permute-start(f32[4,32,2048]{2,1,0:T(8,128)S(1)} %get-tuple-element.15), channel_id=1, source_target_pairs={{0,8},{64,72},{8,0},{72,64},{1,9},{65,73},{9,1},{73,65},{2,10},{66... | collective-permute-start | bytes 3145736 | tf_op jit(solution)/shard_map/ppermute | solution.py:35
  93.1 8.7 %shard_map.17.refs_4_ = f32[2048,1024]{1,0:T(8,128)S(1)} custom-call(s32[1]{0:T(128)} %bitcast.core_ref, f32[3,128,2048]{2,1,0:T(8,128)S(1)} %pad_maximum_fusion.refs_0_, f32[1,128,2048]{2,1,0:T(8,128)S(1)} %constant_dynamic-update-slice_fusion.refs_1_, f32[3,128,2048]{2,1,0:T(8,128)S(1)} %collective-permute-done.11.refs_2_, ...), custom_call_target="tpu_custom_call" | custom-call | flops 6442450944 | bytes 16777216 | tf_op jit(solution)/shard_map/pallas_call | solution.py:106
  101.8 0.7 collective-permute-done.26
  102.5 0.3 pad_maximum_fusion.2.refs_0_
  103.1 9.7 %collective-permute-done.6 = f32[4,32,2048]{2,1,0:T(8,128)S(1)} collective-permute-done((f32[4,32,2048]{2,1,0:T(8,128)S(1)}, f32[4,32,2048]{2,1,0:T(8,128)S(1)}, u32[]{:S(2)}, u32[]{:S(2)}) %collective-permute-start.6) | collective-permute-done | bytes 1048608 | tf_op jit(solution)/shard_map/ppermute | solution.py:35
  112.8 0.8 collective-permute-start.13
  113.6 2.5 %collective-permute-start.14 = (f32[1,128,2048]{2,1,0:T(8,128)S(1)}, f32[1,128,2048]{2,1,0:T(8,128)S(1)}, u32[]{:S(2)}, u32[]{:S(2)}) collective-permute-start(f32[1,128,2048]{2,1,0:T(8,128)S(1)} %bitcast.42), channel_id=1, source_target_pairs={{0,48},{1,7},{2,50},{3,1},{4,52},{5,3},{6,54},{7,5},{16,0},{17,23}... | collective-permute-start | bytes 3145736 | tf_op jit(solution)/shard_map/ppermute | solution.py:29
  116.3 3.2 %collective-permute-start.28 = (f32[1,64,2048]{2,1,0:T(8,128)S(1)}, f32[1,64,2048]{2,1,0:T(8,128)S(1)}, u32[]{:S(2)}, u32[]{:S(2)}) collective-permute-start(f32[1,64,2048]{2,1,0:T(8,128)S(1)} %slice.47), channel_id=1, source_target_pairs={{0,48},{1,7},{2,50},{3,1},{4,52},{5,3},{6,54},{7,5},{16,0},{17,23}... | collective-permute-start | bytes 1572872 | tf_op jit(solution)/shard_map/ppermute | solution.py:29
  119.5 8.8 %shard_map.18.refs_4_ = f32[2048,1024]{1,0:T(8,128)S(1)} custom-call(s32[1]{0:T(128)} %bitcast.core_ref, f32[3,128,2048]{2,1,0:T(8,128)S(1)} %pad_maximum_fusion.1.refs_0_, f32[1,128,2048]{2,1,0:T(8,128)S(1)} %constant_dynamic-update-slice_fusion.2.refs_1_, f32[3,128,2048]{2,1,0:T(8,128)S(1)} %collective-permute-done.21.refs_2_, ...), custom_call_target="tpu_custom_call", output_to_operand_aliasing={{}: (5, {})} | custom-call | flops 6442450944 | bytes 16777216 | tf_op jit(solution)/shard_map/pallas_call | solution.py:106
  128.3 6.2 %collective-permute-done.27 = f32[1,64,2048]{2,1,0:T(8,128)S(1)} collective-permute-done((f32[1,64,2048]{2,1,0:T(8,128)S(1)}, f32[1,64,2048]{2,1,0:T(8,128)S(1)}, u32[]{:S(2)}, u32[]{:S(2)}) %collective-permute-start.27) | collective-permute-done | bytes 524320 | tf_op jit(solution)/shard_map/ppermute | solution.py:29
  134.8 0.6 collective-permute-start.31
  135.5 1.5 collective-permute-start.23
  137.0 1.9 %collective-permute-start.24 = (f32[1,64,2048]{2,1,0:T(8,128)S(1)}, f32[1,64,2048]{2,1,0:T(8,128)S(1)}, u32[]{:S(2)}, u32[]{:S(2)}) collective-permute-start(f32[1,64,2048]{2,1,0:T(8,128)S(1)} %slice.45), channel_id=1, source_target_pairs={{0,48},{1,7},{2,50},{3,1},{4,52},{5,3},{6,54},{7,5},{16,0},{17,23}... | collective-permute-start | bytes 1572872 | tf_op jit(solution)/shard_map/ppermute | solution.py:29
  138.9 8.8 %shard_map.19.refs_4_ = f32[2048,1024]{1,0:T(8,128)S(1)} custom-call(s32[1]{0:T(128)} %bitcast.core_ref, f32[3,128,2048]{2,1,0:T(8,128)S(1)} %pad_maximum_fusion.2.refs_0_, f32[1,128,2048]{2,1,0:T(8,128)S(1)} %constant_dynamic-update-slice_fusion.7.refs_1_, f32[3,128,2048]{2,1,0:T(8,128)S(1)} %collective-permute-done.29.refs_2_, ...), custom_call_target="tpu_custom_call", output_to_operand_aliasing={{}: (5, {})} | custom-call | flops 6442450944 | bytes 16777216 | tf_op jit(solution)/shard_map/pallas_call | solution.py:106
  147.9 2.6 %collective-permute-done.32.refs_3_ = f32[1,128,2048]{2,1,0:T(8,128)S(1)} collective-permute-done((f32[1,128,2048]{2,1,0:T(8,128)S(1)}, f32[1,128,2048]{2,1,0:T(8,128)S(1)}, u32[]{:S(2)}, u32[]{:S(2)}) %collective-permute-start.32) | collective-permute-done | bytes 1048608 | tf_op jit(solution)/shard_map/ppermute | solution.py:39
  150.6 9.9 %shard_map.20 = f32[2048,1024]{1,0:T(8,128)} custom-call(s32[1]{0:T(128)} %bitcast.core_ref, f32[3,128,2048]{2,1,0:T(8,128)S(1)} %constant_dynamic-update-slice_fusion.4.refs_0_, f32[1,128,2048]{2,1,0:T(8,128)S(1)} %constant_dynamic-update-slice_fusion.9.refs_1_, f32[3,128,2048]{2,1,0:T(8,128)S(1)} %collective-permute-done.31.refs_2_, ...), custom_call_target="tpu_custom_call" | custom-call | flops 6442450944 | bytes 16777216 | tf_op jit(solution)/shard_map/pallas_call | solution.py:106
  (57 shorter events, 2.7 us)
Async XLA Ops:
  0.0 2.9 %collective-permute-start = (f32[16,16384]{1,0:T(8,128)}, f32[16,16384]{1,0:T(8,128)S(1)}, u32[]{:S(2)}, u32[]{:S(2)}) collective-permute-start(f32[16,16384]{1,0:T(8,128)} %param.1), channel_id=1, source_target_pairs={{0,1},{1,0},{2,3},{3,2},{4,5},{5,4},{6,7},{7,6},{8,9},{9,8},{10,11... | collective-permute-start | bytes 3145736 | tf_op jit(solution)/shard_map/ppermute | solution.py:39
  4.4 10.5 %collective-permute-start.1 = (f32[2,32,2048]{2,1,0:T(8,128)S(1)}, f32[2,32,2048]{2,1,0:T(8,128)S(1)}, u32[]{:S(2)}, u32[]{:S(2)}) collective-permute-start(f32[2,32,2048]{2,1,0:T(8,128)S(1)} %pad_maximum_fusion.6), channel_id=1, source_target_pairs={{0,2},{1,17},{2,4},{3,19},{4,6},{5,21},{6,0},{7,23},{16,18},{17,33... | collective-permute-start | bytes 1572872 | tf_op jit(solution)/shard_map/ppermute | solution.py:20
  6.2 9.2 %collective-permute-start.2 = (f32[2,32,2048]{2,1,0:T(8,128)S(1)}, f32[2,32,2048]{2,1,0:T(8,128)S(1)}, u32[]{:S(2)}, u32[]{:S(2)}) collective-permute-start(f32[2,32,2048]{2,1,0:T(8,128)S(1)} %pad_maximum_fusion.7), channel_id=1, source_target_pairs={{0,6},{1,49},{2,0},{3,51},{4,2},{5,53},{6,4},{7,55},{16,22},{17,1}... | collective-permute-start | bytes 1572872 | tf_op jit(solution)/shard_map/ppermute | solution.py:20
  7.9 14.0 %collective-permute-start.3 = (f32[2,32,2048]{2,1,0:T(8,128)S(1)}, f32[2,32,2048]{2,1,0:T(8,128)}, u32[]{:S(2)}, u32[]{:S(2)}) collective-permute-start(f32[2,32,2048]{2,1,0:T(8,128)S(1)} %pad_maximum_fusion.8), channel_id=1, source_target_pairs={{0,4},{1,33},{2,6},{3,35},{4,0},{5,37},{6,2},{7,39},{16,20},{17,49... | collective-permute-start | bytes 1572872 | tf_op jit(solution)/shard_map/ppermute | solution.py:20
  23.7 16.9 %collective-permute-start.7 = (f32[1,128,2048]{2,1,0:T(8,128)S(1)}, f32[1,128,2048]{2,1,0:T(8,128)S(1)}, u32[]{:S(2)}, u32[]{:S(2)}) collective-permute-start(f32[1,128,2048]{2,1,0:T(8,128)S(1)} %bitcast.32), channel_id=1, source_target_pairs={{0,16},{1,3},{2,18},{3,5},{4,20},{5,7},{6,22},{7,1},{16,32},{17,19... | collective-permute-start | bytes 3145736 | tf_op jit(solution)/shard_map/ppermute | solution.py:29
  25.7 14.9 %collective-permute-start.8 = (f32[1,128,2048]{2,1,0:T(8,128)S(1)}, f32[1,128,2048]{2,1,0:T(8,128)S(1)}, u32[]{:S(2)}, u32[]{:S(2)}) collective-permute-start(f32[1,128,2048]{2,1,0:T(8,128)S(1)} %bitcast.33), channel_id=1, source_target_pairs={{0,48},{1,7},{2,50},{3,1},{4,52},{5,3},{6,54},{7,5},{16,0},{17,23}... | collective-permute-start | bytes 3145736 | tf_op jit(solution)/shard_map/ppermute | solution.py:29
  27.9 13.8 %collective-permute-start.15 = (f32[4,16,2048]{2,1,0:T(8,128)S(1)}, f32[4,16,2048]{2,1,0:T(8,128)S(1)}, u32[]{:S(2)}, u32[]{:S(2)}) collective-permute-start(f32[4,16,2048]{2,1,0:T(8,128)S(1)} %get-tuple-element.39), channel_id=1, source_target_pairs={{0,64},{64,8},{8,72},{72,0},{1,65},{65,9},{9,73},{73,1},{2,66},{66... | collective-permute-start | bytes 1572872 | tf_op jit(solution)/shard_map/ppermute | solution.py:35
  29.6 12.3 %collective-permute-start.16 = (f32[4,16,2048]{2,1,0:T(8,128)S(1)}, f32[4,16,2048]{2,1,0:T(8,128)S(1)}, u32[]{:S(2)}, u32[]{:S(2)}) collective-permute-start(f32[4,16,2048]{2,1,0:T(8,128)S(1)} %get-tuple-element.41), channel_id=1, source_target_pairs={{0,72},{64,0},{8,64},{72,8},{1,73},{65,1},{9,65},{73,9},{2,74},{66... | collective-permute-start | bytes 1572872 | tf_op jit(solution)/shard_map/ppermute | solution.py:35
  40.9 52.3 %collective-permute-start.11 = (f32[3,128,2048]{2,1,0:T(8,128)S(1)}, f32[3,128,2048]{2,1,0:T(8,128)S(1)}, u32[]{:S(2)}, u32[]{:S(2)}) collective-permute-start(f32[3,128,2048]{2,1,0:T(8,128)S(1)} %pad_maximum_fusion.refs_0_), channel_id=1, source_target_pairs={{0,1},{1,0},{2,3},{3,2},{4,5},{5,4},{6,7},{7,6},{8,9},{9,8},{10,11... | collective-permute-start | bytes 9437192 | tf_op jit(solution)/shard_map/ppermute | solution.py:39
  42.0 16.1 %collective-permute-start.17 = (f32[1,128,2048]{2,1,0:T(8,128)S(1)}, f32[1,128,2048]{2,1,0:T(8,128)S(1)}, u32[]{:S(2)}, u32[]{:S(2)}) collective-permute-start(f32[1,128,2048]{2,1,0:T(8,128)S(1)} %bitcast.38), channel_id=1, source_target_pairs={{0,16},{1,3},{2,18},{3,5},{4,20},{5,7},{6,22},{7,1},{16,32},{17,19... | collective-permute-start | bytes 3145736 | tf_op jit(solution)/shard_map/ppermute | solution.py:29
  43.5 14.8 %collective-permute-start.18 = (f32[1,128,2048]{2,1,0:T(8,128)S(1)}, f32[1,128,2048]{2,1,0:T(8,128)S(1)}, u32[]{:S(2)}, u32[]{:S(2)}) collective-permute-start(f32[1,128,2048]{2,1,0:T(8,128)S(1)} %bitcast.39), channel_id=1, source_target_pairs={{0,48},{1,7},{2,50},{3,1},{4,52},{5,3},{6,54},{7,5},{16,0},{17,23}... | collective-permute-start | bytes 3145736 | tf_op jit(solution)/shard_map/ppermute | solution.py:29
  45.3 18.4 %collective-permute-start.9 = (f32[1,64,2048]{2,1,0:T(8,128)S(1)}, f32[1,64,2048]{2,1,0:T(8,128)S(1)}, u32[]{:S(2)}, u32[]{:S(2)}) collective-permute-start(f32[1,64,2048]{2,1,0:T(8,128)S(1)} %slice.50), channel_id=1, source_target_pairs={{0,16},{1,3},{2,18},{3,5},{4,20},{5,7},{6,22},{7,1},{16,32},{17,19... | collective-permute-start | bytes 1572872 | tf_op jit(solution)/shard_map/ppermute | solution.py:29
  45.6 21.1 %collective-permute-start.10 = (f32[1,64,2048]{2,1,0:T(8,128)S(1)}, f32[1,64,2048]{2,1,0:T(8,128)S(1)}, u32[]{:S(2)}, u32[]{:S(2)}) collective-permute-start(f32[1,64,2048]{2,1,0:T(8,128)S(1)} %slice.51), channel_id=1, source_target_pairs={{0,48},{1,7},{2,50},{3,1},{4,52},{5,3},{6,54},{7,5},{16,0},{17,23}... | collective-permute-start | bytes 1572872 | tf_op jit(solution)/shard_map/ppermute | solution.py:29
  58.6 57.7 %collective-permute-start.21 = (f32[3,128,2048]{2,1,0:T(8,128)S(1)}, f32[3,128,2048]{2,1,0:T(8,128)S(1)}, u32[]{:S(2)}, u32[]{:S(2)}) collective-permute-start(f32[3,128,2048]{2,1,0:T(8,128)S(1)} %pad_maximum_fusion.1.refs_0_), channel_id=1, source_target_pairs={{0,1},{1,0},{2,3},{3,2},{4,5},{5,4},{6,7},{7,6},{8,9},{9,8},{10,11... | collective-permute-start | bytes 9437192 | tf_op jit(solution)/shard_map/ppermute | solution.py:39
  58.7 15.5 %collective-permute-start.4 = (f32[4,16,2048]{2,1,0:T(8,128)S(1)}, f32[4,16,2048]{2,1,0:T(8,128)S(1)}, u32[]{:S(2)}, u32[]{:S(2)}) collective-permute-start(f32[4,16,2048]{2,1,0:T(8,128)S(1)} %get-tuple-element.40), channel_id=1, source_target_pairs={{0,64},{64,8},{8,72},{72,0},{1,65},{65,9},{9,73},{73,1},{2,66},{66... | collective-permute-start | bytes 1572872 | tf_op jit(solution)/shard_map/ppermute | solution.py:35
  63.7 12.8 %collective-permute-start.5 = (f32[4,16,2048]{2,1,0:T(8,128)S(1)}, f32[4,16,2048]{2,1,0:T(8,128)S(1)}, u32[]{:S(2)}, u32[]{:S(2)}) collective-permute-start(f32[4,16,2048]{2,1,0:T(8,128)S(1)} %get-tuple-element.42), channel_id=1, source_target_pairs={{0,72},{64,0},{8,64},{72,8},{1,73},{65,1},{9,65},{73,9},{2,74},{66... | collective-permute-start | bytes 1572872 | tf_op jit(solution)/shard_map/ppermute | solution.py:35
  66.7 23.6 %collective-permute-start.12 = (f32[1,128,2048]{2,1,0:T(8,128)S(1)}, f32[1,128,2048]{2,1,0:T(8,128)S(1)}, u32[]{:S(2)}, u32[]{:S(2)}) collective-permute-start(f32[1,128,2048]{2,1,0:T(8,128)S(1)} %constant_dynamic-update-slice_fusion.refs_1_), channel_id=1, source_target_pairs={{0,1},{1,0},{2,3},{3,2},{4,5},{5,4},{6,7},{7,6},{8,9},{9,8},{10,11... | collective-permute-start | bytes 3145736 | tf_op jit(solution)/shard_map/ppermute | solution.py:39
  74.2 10.4 %collective-permute-start.19 = (f32[1,64,2048]{2,1,0:T(8,128)S(1)}, f32[1,64,2048]{2,1,0:T(8,128)S(1)}, u32[]{:S(2)}, u32[]{:S(2)}) collective-permute-start(f32[1,64,2048]{2,1,0:T(8,128)S(1)} %slice.54), channel_id=1, source_target_pairs={{0,16},{1,3},{2,18},{3,5},{4,20},{5,7},{6,22},{7,1},{16,32},{17,19... | collective-permute-start | bytes 1572872 | tf_op jit(solution)/shard_map/ppermute | solution.py:29
  76.5 10.0 %collective-permute-start.20 = (f32[1,64,2048]{2,1,0:T(8,128)S(1)}, f32[1,64,2048]{2,1,0:T(8,128)S(1)}, u32[]{:S(2)}, u32[]{:S(2)}) collective-permute-start(f32[1,64,2048]{2,1,0:T(8,128)S(1)} %slice.55), channel_id=1, source_target_pairs={{0,48},{1,7},{2,50},{3,1},{4,52},{5,3},{6,54},{7,5},{16,0},{17,23}... | collective-permute-start | bytes 1572872 | tf_op jit(solution)/shard_map/ppermute | solution.py:29
  84.6 17.2 %collective-permute-start.25 = (f32[1,128,2048]{2,1,0:T(8,128)S(1)}, f32[1,128,2048]{2,1,0:T(8,128)S(1)}, u32[]{:S(2)}, u32[]{:S(2)}) collective-permute-start(f32[1,128,2048]{2,1,0:T(8,128)S(1)} %bitcast.35), channel_id=1, source_target_pairs={{0,16},{1,3},{2,18},{3,5},{4,20},{5,7},{6,22},{7,1},{16,32},{17,19... | collective-permute-start | bytes 3145736 | tf_op jit(solution)/shard_map/ppermute | solution.py:29
  86.5 16.0 %collective-permute-start.26 = (f32[1,128,2048]{2,1,0:T(8,128)S(1)}, f32[1,128,2048]{2,1,0:T(8,128)S(1)}, u32[]{:S(2)}, u32[]{:S(2)}) collective-permute-start(f32[1,128,2048]{2,1,0:T(8,128)S(1)} %bitcast.36), channel_id=1, source_target_pairs={{0,48},{1,7},{2,50},{3,1},{4,52},{5,3},{6,54},{7,5},{16,0},{17,23}... | collective-permute-start | bytes 3145736 | tf_op jit(solution)/shard_map/ppermute | solution.py:29
  90.3 22.5 %collective-permute-start.6 = (f32[4,32,2048]{2,1,0:T(8,128)S(1)}, f32[4,32,2048]{2,1,0:T(8,128)S(1)}, u32[]{:S(2)}, u32[]{:S(2)}) collective-permute-start(f32[4,32,2048]{2,1,0:T(8,128)S(1)} %get-tuple-element.15), channel_id=1, source_target_pairs={{0,8},{64,72},{8,0},{72,64},{1,9},{65,73},{9,1},{73,65},{2,10},{66... | collective-permute-start | bytes 3145736 | tf_op jit(solution)/shard_map/ppermute | solution.py:35
  93.1 23.0 %collective-permute-start.22 = (f32[1,128,2048]{2,1,0:T(8,128)S(1)}, f32[1,128,2048]{2,1,0:T(8,128)S(1)}, u32[]{:S(2)}, u32[]{:S(2)}) collective-permute-start(f32[1,128,2048]{2,1,0:T(8,128)S(1)} %constant_dynamic-update-slice_fusion.2.refs_1_), channel_id=1, source_target_pairs={{0,1},{1,0},{2,3},{3,2},{4,5},{5,4},{6,7},{7,6},{8,9},{9,8},{10,11... | collective-permute-start | bytes 3145736 | tf_op jit(solution)/shard_map/ppermute | solution.py:39
  102.9 36.0 %collective-permute-start.29 = (f32[3,128,2048]{2,1,0:T(8,128)S(1)}, f32[3,128,2048]{2,1,0:T(8,128)S(1)}, u32[]{:S(2)}, u32[]{:S(2)}) collective-permute-start(f32[3,128,2048]{2,1,0:T(8,128)S(1)} %pad_maximum_fusion.2.refs_0_), channel_id=1, source_target_pairs={{0,1},{1,0},{2,3},{3,2},{4,5},{5,4},{6,7},{7,6},{8,9},{9,8},{10,11... | collective-permute-start | bytes 9437192 | tf_op jit(solution)/shard_map/ppermute | solution.py:39
  112.8 21.9 %collective-permute-start.13 = (f32[1,128,2048]{2,1,0:T(8,128)S(1)}, f32[1,128,2048]{2,1,0:T(8,128)S(1)}, u32[]{:S(2)}, u32[]{:S(2)}) collective-permute-start(f32[1,128,2048]{2,1,0:T(8,128)S(1)} %bitcast.41), channel_id=1, source_target_pairs={{0,16},{1,3},{2,18},{3,5},{4,20},{5,7},{6,22},{7,1},{16,32},{17,19... | collective-permute-start | bytes 3145736 | tf_op jit(solution)/shard_map/ppermute | solution.py:29
  113.6 21.1 %collective-permute-start.14 = (f32[1,128,2048]{2,1,0:T(8,128)S(1)}, f32[1,128,2048]{2,1,0:T(8,128)S(1)}, u32[]{:S(2)}, u32[]{:S(2)}) collective-permute-start(f32[1,128,2048]{2,1,0:T(8,128)S(1)} %bitcast.42), channel_id=1, source_target_pairs={{0,48},{1,7},{2,50},{3,1},{4,52},{5,3},{6,54},{7,5},{16,0},{17,23}... | collective-permute-start | bytes 3145736 | tf_op jit(solution)/shard_map/ppermute | solution.py:29
  116.2 18.3 %collective-permute-start.27 = (f32[1,64,2048]{2,1,0:T(8,128)S(1)}, f32[1,64,2048]{2,1,0:T(8,128)S(1)}, u32[]{:S(2)}, u32[]{:S(2)}) collective-permute-start(f32[1,64,2048]{2,1,0:T(8,128)S(1)} %slice.46), channel_id=1, source_target_pairs={{0,16},{1,3},{2,18},{3,5},{4,20},{5,7},{6,22},{7,1},{16,32},{17,19... | collective-permute-start | bytes 1572872 | tf_op jit(solution)/shard_map/ppermute | solution.py:29
  116.3 18.2 %collective-permute-start.28 = (f32[1,64,2048]{2,1,0:T(8,128)S(1)}, f32[1,64,2048]{2,1,0:T(8,128)S(1)}, u32[]{:S(2)}, u32[]{:S(2)}) collective-permute-start(f32[1,64,2048]{2,1,0:T(8,128)S(1)} %slice.47), channel_id=1, source_target_pairs={{0,48},{1,7},{2,50},{3,1},{4,52},{5,3},{6,54},{7,5},{16,0},{17,23}... | collective-permute-start | bytes 1572872 | tf_op jit(solution)/shard_map/ppermute | solution.py:29
  134.6 4.3 %collective-permute-start.30 = (f32[1,128,2048]{2,1,0:T(8,128)S(1)}, f32[1,128,2048]{2,1,0:T(8,128)S(1)}, u32[]{:S(2)}, u32[]{:S(2)}) collective-permute-start(f32[1,128,2048]{2,1,0:T(8,128)S(1)} %constant_dynamic-update-slice_fusion.7.refs_1_), channel_id=1, source_target_pairs={{0,1},{1,0},{2,3},{3,2},{4,5},{5,4},{6,7},{7,6},{8,9},{9,8},{10,11... | collective-permute-start | bytes 3145736 | tf_op jit(solution)/shard_map/ppermute | solution.py:39
  134.8 15.7 %collective-permute-start.31 = (f32[3,128,2048]{2,1,0:T(8,128)S(1)}, f32[3,128,2048]{2,1,0:T(8,128)S(1)}, u32[]{:S(2)}, u32[]{:S(2)}) collective-permute-start(f32[3,128,2048]{2,1,0:T(8,128)S(1)} %constant_dynamic-update-slice_fusion.4.refs_0_), channel_id=1, source_target_pairs={{0,1},{1,0},{2,3},{3,2},{4,5},{5,4},{6,7},{7,6},{8,9},{9,8},{10,11... | collective-permute-start | bytes 9437192 | tf_op jit(solution)/shard_map/ppermute | solution.py:39
  135.5 12.2 %collective-permute-start.23 = (f32[1,64,2048]{2,1,0:T(8,128)S(1)}, f32[1,64,2048]{2,1,0:T(8,128)S(1)}, u32[]{:S(2)}, u32[]{:S(2)}) collective-permute-start(f32[1,64,2048]{2,1,0:T(8,128)S(1)} %slice.44), channel_id=1, source_target_pairs={{0,16},{1,3},{2,18},{3,5},{4,20},{5,7},{6,22},{7,1},{16,32},{17,19... | collective-permute-start | bytes 1572872 | tf_op jit(solution)/shard_map/ppermute | solution.py:29
  137.0 10.8 %collective-permute-start.24 = (f32[1,64,2048]{2,1,0:T(8,128)S(1)}, f32[1,64,2048]{2,1,0:T(8,128)S(1)}, u32[]{:S(2)}, u32[]{:S(2)}) collective-permute-start(f32[1,64,2048]{2,1,0:T(8,128)S(1)} %slice.45), channel_id=1, source_target_pairs={{0,48},{1,7},{2,50},{3,1},{4,52},{5,3},{6,54},{7,5},{16,0},{17,23}... | collective-permute-start | bytes 1572872 | tf_op jit(solution)/shard_map/ppermute | solution.py:29
  147.8 2.7 %collective-permute-start.32 = (f32[1,128,2048]{2,1,0:T(8,128)S(1)}, f32[1,128,2048]{2,1,0:T(8,128)S(1)}, u32[]{:S(2)}, u32[]{:S(2)}) collective-permute-start(f32[1,128,2048]{2,1,0:T(8,128)S(1)} %constant_dynamic-update-slice_fusion.9.refs_1_), channel_id=1, source_target_pairs={{0,1},{1,0},{2,3},{3,2},{4,5},{5,4},{6,7},{7,6},{8,9},{9,8},{10,11... | collective-permute-start | bytes 3145736 | tf_op jit(solution)/shard_map/ppermute | solution.py:39
